TPU v7x, 256 devices: a whole 4x4x8 slice. The times are simulated.
256 devices in a mesh: gx: 8 (over x, core), gy: 32 (over y, z).
Axes of the slice: x: 4, y: 4, z: 8, core: 2. Of those that a mesh axis runs over, the one named last changes fastest.
Arguments:
- rock_type: int32 [128, 1024, 256], P('gx', 'gy'), may hold values from 0 to 7
- perm_table: float32 [8], replicated, may hold values from 0.1 to 10
- poro_table: float32 [8], replicated, may hold values from 0.1 to 0.3
- saturation: float32 [128, 1024, 256], P('gx', 'gy'), may hold values from 0 to 1
- pressure_old: float32 [128, 1024, 256], P('gx', 'gy'), may hold values from -10 to 10
- factor_inverse: float32 [8, 64, 256, 256], P('gx', 'gy'), may hold values from -2 to 2, as said below
- inject_cells: int32 [4, 128, 2], replicated, may hold values from 0 to 131071, as said below
- inject_index: float32 [4, 128], replicated, may hold values from 1 to 8
- inject_rate: float32 [4], replicated, may hold values from 200 to 1000
- produce_cells: int32 [8, 128, 2], replicated, may hold values from 0 to 131071, as said below
- produce_index: float32 [8, 128], replicated, may hold values from 1 to 8
- produce_pressure: float32 [8], replicated, may hold values from -3 to -1
Outputs:
- saturation_new: float32 [128, 1024, 256], P('gx', 'gy')
- pressure: float32 [128, 1024, 256], P('gx', 'gy')
Inputs may be any that keep to these rules, and one draw needn't show every extreme that they name: `inject_cells`: the 128 perforations of a well lie in one layer and one row of columns: perforation k at second index (start + k) modulo 1024 for a start per well. `produce_cells`: laid out as for injectors. `factor_inverse`: each block's matrix is lower triangular with a positive diagonal.
All inputs are finite; a program needn't handle non-finite values.
Results may differ from a plain program's by a relative error of at most 0.0003.
Values sent between devices are 32-bit elements; how exact they have to be, the bound alone decides.
A program may use at most 64 MiB of HBM per device.

v0:
```python
import jax
import jax.numpy as jnp
from jax import lax
from jax.sharding import PartitionSpec as P

BLOCK = 16
ITERS = 3


water_viscosity = 0.5
oil_viscosity = 1.0
time_step = 0.002
compress = 1.0
vertical_ratio = 0.1


def extended(block, sides, width):
    for axis, dim in sides:
        count = lax.axis_size(axis)
        forward = [(i, i + 1) for i in range(count - 1)]
        backward = [(target, source) for source, target in forward]
        low = lax.ppermute(
            lax.slice_in_dim(block, block.shape[dim] - width, None, axis=dim), axis, forward
        )
        high = lax.ppermute(lax.slice_in_dim(block, 0, width, axis=dim), axis, backward)
        block = jnp.concatenate([low, block, high], axis=dim)
    return block


def total_mobility(saturation):
    return (
        saturation * saturation / water_viscosity
        + (1.0 - saturation) * (1.0 - saturation) / oil_viscosity
    )


def mobilities(saturation):
    water_part = saturation * saturation / water_viscosity
    total_part = water_part + (1.0 - saturation) * (1.0 - saturation) / oil_viscosity
    return (total_part, water_part / total_part)


def harmonic(former, latter):
    summed = former + latter
    safe_sum = jnp.where(summed > 0.0, summed, 1.0)
    return 2.0 * former * latter / safe_sum


def table_lookup(rock_type, table_values):
    looked = jnp.zeros(rock_type.shape, jnp.float32)
    for rock_entry in range(table_values.shape[0]):
        looked = looked + jnp.where(rock_type == rock_entry, table_values[rock_entry], 0.0)
    return looked


def perf_slots(cells, margin, row_count, col_count, layer_count, row_start, col_start, full_cols):
    column = cells[..., 0]
    layer_index = cells[..., 1]
    local_row = column // full_cols - row_start + margin
    local_col = column % full_cols - col_start + margin
    wide_rows = row_count + 2 * margin
    wide_cols = col_count + 2 * margin
    inside = (local_row >= 0) & (local_row < wide_rows) & (local_col >= 0) & (local_col < wide_cols)
    owned_here = (
        (local_row >= margin)
        & (local_row < margin + row_count)
        & (local_col >= margin)
        & (local_col < margin + col_count)
    )
    slot_index = jnp.where(
        inside, (local_row * wide_cols + local_col) * layer_count + layer_index, 0
    )
    return (slot_index, inside, owned_here)


def spread(slot_index, inside, values, grid_shape):
    flat_field = jnp.zeros((grid_shape[0] * grid_shape[1] * grid_shape[2],), jnp.float32)
    flat_field = flat_field.at[slot_index.reshape(-1)].add(
        jnp.where(inside, values, 0.0).reshape(-1)
    )
    return flat_field.reshape(grid_shape)


def pick(field_values, slot_index):
    return field_values.reshape(-1)[slot_index]


def layer_difference(flux_values):
    zero_layer = jnp.zeros_like(flux_values[:, :, :1])
    return jnp.concatenate([flux_values, zero_layer], 2) - jnp.concatenate(
        [zero_layer, flux_values], 2
    )


def apply_padded(padded, vector, coefficients):
    coef_x, coef_y, coef_z, diagonal = coefficients
    across_x = coef_x * (padded[:-1, 1:-1] - padded[1:, 1:-1])
    across_y = coef_y * (padded[1:-1, :-1] - padded[1:-1, 1:])
    across_z = coef_z * (vector[:, :, :-1] - vector[:, :, 1:])
    return (
        diagonal * vector
        + across_x[1:]
        - across_x[:-1]
        + across_y[:, 1:]
        - across_y[:, :-1]
        + layer_difference(across_z)
    )


def precondition(vector, factor_inverse):
    row_count, col_count, layer_count = vector.shape
    blocks = vector.reshape(row_count // BLOCK, BLOCK, col_count // BLOCK, BLOCK, layer_count)
    lowered = jnp.einsum(
        "aibjk,abmk->aibjm", blocks, factor_inverse, precision=lax.Precision.HIGHEST
    )
    result = jnp.einsum(
        "aibjm,abmk->aibjk", lowered, factor_inverse, precision=lax.Precision.HIGHEST
    )
    return result.reshape(vector.shape)


def per_device(
    rock_type,
    perm_table,
    poro_table,
    saturation,
    pressure_old,
    factor_inverse,
    inject_cells,
    inject_index,
    inject_rate,
    produce_cells,
    produce_index,
    produce_pressure,
):
    row_count, col_count, layer_count = saturation.shape
    full_cols = col_count * lax.axis_size("gy")
    row_start = lax.axis_index("gx") * row_count
    col_start = lax.axis_index("gy") * col_count
    permeability = table_lookup(rock_type, perm_table)
    porosity = table_lookup(rock_type, poro_table)
    margin = 0
    padded = extended(
        jnp.stack([saturation, pressure_old, permeability]), (("gx", 1), ("gy", 2)), 1
    )
    saturation_pad = padded[0]
    pressure_pad = padded[1]
    permeability_pad = padded[2]

    def locate(cells, edge_cells):
        return perf_slots(
            cells, edge_cells, row_count, col_count, layer_count, row_start, col_start, full_cols
        )

    total_pad, fraction_pad = mobilities(saturation_pad)
    saturation_region = saturation_pad[1:-1, 1:-1]
    pressure_region = pressure_pad[1:-1, 1:-1]
    total_region = total_pad[1:-1, 1:-1]
    fraction_region = fraction_pad[1:-1, 1:-1]
    region_shape = saturation_region.shape
    inject_slot, inject_inside, inject_owned = locate(inject_cells, margin)
    inject_weight = inject_index * pick(total_region, inject_slot)
    own_sums = jnp.sum(jnp.where(inject_owned, inject_weight, 0.0), axis=1)
    well_sums = lax.psum(own_sums, ("gx", "gy"))
    inject_share = inject_rate[:, None] * inject_weight / well_sums[:, None]
    inject_source = spread(inject_slot, inject_inside, inject_share, region_shape)
    produce_slot, produce_inside, produce_owned = locate(produce_cells, margin)
    produce_flow = (
        produce_index
        * pick(total_region, produce_slot)
        * (pick(pressure_region, produce_slot) - produce_pressure[:, None])
    )
    produce_water = spread(
        produce_slot,
        produce_inside,
        produce_flow * pick(fraction_region, produce_slot),
        region_shape,
    )
    vertical = vertical_ratio * permeability_pad[1:-1, 1:-1]
    face_x = harmonic(permeability_pad[:-1, 1:-1], permeability_pad[1:, 1:-1])
    face_y = harmonic(permeability_pad[1:-1, :-1], permeability_pad[1:-1, 1:])
    face_z = harmonic(vertical[:, :, :-1], vertical[:, :, 1:])
    flow_x = face_x * (pressure_pad[:-1, 1:-1] - pressure_pad[1:, 1:-1])
    water_x = flow_x * jnp.where(flow_x > 0.0, fraction_pad[:-1, 1:-1], fraction_pad[1:, 1:-1])
    flow_y = face_y * (pressure_pad[1:-1, :-1] - pressure_pad[1:-1, 1:])
    water_y = flow_y * jnp.where(flow_y > 0.0, fraction_pad[1:-1, :-1], fraction_pad[1:-1, 1:])
    flow_z = face_z * (pressure_region[:, :, :-1] - pressure_region[:, :, 1:])
    water_z = flow_z * jnp.where(
        flow_z > 0.0, fraction_region[:, :, :-1], fraction_region[:, :, 1:]
    )
    divergence = (
        water_x[1:] - water_x[:-1] + water_y[:, 1:] - water_y[:, :-1] + layer_difference(water_z)
    )
    safe_porosity = jnp.where(porosity > 0.0, porosity, 1.0)
    saturation_region_new = saturation_region - time_step / safe_porosity * (
        divergence + produce_water - inject_source
    )
    total_region_new = total_mobility(saturation_region_new)
    total_new_pad = extended(total_region_new, (("gx", 0), ("gy", 1)), 1)
    total_new = total_new_pad[1:-1, 1:-1]
    coef_x = face_x * (0.5 * (total_new_pad[:-1, 1:-1] + total_new_pad[1:, 1:-1]))
    coef_y = face_y * (0.5 * (total_new_pad[1:-1, :-1] + total_new_pad[1:-1, 1:]))
    coef_z = face_z * (0.5 * (total_new[:, :, :-1] + total_new[:, :, 1:]))
    own_slot, own_inside, own_unused = locate(produce_cells, 0)
    produce_coef = produce_index * pick(total_new, own_slot)
    grid_shape = saturation.shape
    diagonal = compress * porosity + spread(own_slot, own_inside, produce_coef, grid_shape)
    right_side = (
        compress * porosity * pressure_old
        + inject_source
        + spread(own_slot, own_inside, produce_coef * produce_pressure[:, None], grid_shape)
    )
    coefficients = (coef_x, coef_y, coef_z, diagonal)
    residual = right_side - apply_padded(pressure_pad, pressure_old, coefficients)
    solution = pressure_old

    def residual_product(residual_now):
        precond_now = precondition(residual_now, factor_inverse)
        return (precond_now, lax.psum(jnp.sum(residual_now * precond_now), ("gx", "gy")))

    precond, product = residual_product(residual)
    direction = precond
    for sweep in range(ITERS):
        padded_vector = extended(direction, (("gx", 0), ("gy", 1)), 1)
        image_field = apply_padded(padded_vector, direction, coefficients)
        step_size = product / lax.psum(jnp.sum(direction * image_field), ("gx", "gy"))
        solution = solution + step_size * direction
        if sweep + 1 < ITERS:
            residual = residual - step_size * image_field
            precond, product_next = residual_product(residual)
            direction = precond + product_next / product * direction
            product = product_next
    return (saturation_region_new, solution)


def solution(mesh):
    in_specs = (
        P("gx", "gy", None),
        P(),
        P(),
        P("gx", "gy", None),
        P("gx", "gy", None),
        P("gx", "gy", None, None),
        P(),
        P(),
        P(),
        P(),
        P(),
        P(),
    )
    out_specs = (P("gx", "gy", None), P("gx", "gy", None))
    return jax.shard_map(
        per_device, mesh=mesh, in_specs=in_specs, out_specs=out_specs, check_vma=False
    )
```

profile of v0, /device:TPU:1, one launch (start us, length us, event | category | flops | bytes accessed | tf_op | source)
XLA Modules:
  0.0 650.9 jit_solution(5346834001334372657)
XLA Ops:
  2.3 7.7 %add_bitcast_fusion = (f32[1,16,32,256]{3,2,1,0:T(8,128)S(1)}, pred[16,32,256]{2,1,0:T(8,128)(4,1)S(1)}, pred[16,32,256]{2,1,0:T(8,128)(4,1)S(1)}, pred[16,32,25...) fusion(f32[]{:T(128)} %bitcast.9, f32[]{:T(128)} %bitcast.8, ...), kind=kLoop, calls=%fused_computation.145 | loop fusion | flops 3014656 | bytes 2097184 | tf_op jit(solution)/shard_map/stack | solution.py:144
  10.0 5.1 collective-permute-start.1
  20.0 4.0 collective-permute-start.2
  35.5 83.6 %psum.49 = f32[4]{0:T(128)S(1)} all-reduce(f32[4]{0:T(128)S(1)} %get-tuple-element.20), channel_id=1, replica_groups=mesh['gx'=8,'gy'=32] {'gx','gy'}, use_global_device_ids=true, to_apply=%region_2.3 | all-reduce | flops 4 | bytes 32 | tf_op jit(solution)/shard_map/psum | solution.py:164
  119.2 4.2 scatter_custom_fusion.1
  125.7 6.2 gather_fusion
  131.9 6.2 gather_fusion.2
  139.4 6.2 gather_fusion.1
  146.4 8.4 %scatter_custom_fusion = f32[131072]{0:T(1024)} fusion(s32[1024]{0:T(1024)S(1)} %bitcast.241, f32[1024]{0:T(1024)S(1)} %fusion.67, f32[]{:T(128)} %constant.47.clone.1), kind=kCustom, calls=%fused_computation.152 | custom fusion | flops 1024 | bytes 524292 | tf_op jit(solution)/shard_map/scatter-add | solution.py:78
  158.7 8.0 %multiply_add_fusion.4 = (f32[16,32,256]{2,1,0:T(8,128)S(1)}, f32[16,32,256]{2,1,0:T(8,128)}, f32[16,32,256]{2,1,0:T(8,128)}) fusion(f32[16,32,256]{2,1,0:T(8,128)S(1)} %copy-done.20, f32[16,32,256]{2,1,0:T(8,128)S(1)} %copy-done.28, f32[16,32,255]{2,1,0:T(8,128)S(1)} %fusion.35, f32[16,33,256]{2,1,0:T(8,128)S(1)} %copy-done.23, ...), kind=kLoop, calls=%fused_computation.143 | loop fusion | flops 4194304 | bytes 6813728 | tf_op jit(solution)/shard_map/add | solution.py:32
  170.7 3.3 collective-permute-start.4
  174.3 6.2 gather_fusion.4
  180.5 7.8 %scatter_custom_fusion.2 = f32[131072]{0:T(1024)S(1)} fusion(s32[1024]{0:T(1024)S(1)} %bitcast.242, f32[1024]{0:T(1024)S(1)} %get-tuple-element.57, f32[]{:T(128)} %constant.47.clone.1), kind=kCustom, calls=%fused_computation.148 | custom fusion | flops 1024 | bytes 524292 | tf_op jit(solution)/shard_map/scatter-add | solution.py:78
  189.2 7.8 %scatter_custom_fusion.3 = f32[131072]{0:T(1024)S(1)} fusion(s32[1024]{0:T(1024)S(1)} %bitcast.243, f32[1024]{0:T(1024)S(1)} %get-tuple-element.56, f32[]{:T(128)} %constant.47.clone.1), kind=kCustom, calls=%fused_computation.146 | custom fusion | flops 1024 | bytes 524292 | tf_op jit(solution)/shard_map/scatter-add | solution.py:78
  199.3 4.3 collective-permute-start.6
  210.1 3.6 collective-permute-start.8
  216.1 4.0 collective-permute-start.10
  222.2 80.8 %all-reduce.10 = (f32[]{:T(128)}, f32[]{:T(128)}) all-reduce(f32[]{:T(128)} %get-tuple-element.3, f32[]{:T(128)} %get-tuple-element.2), channel_id=1, replica_groups=mesh['gx'=8,'gy'=32] {'gx','gy'}, use_global_device_ids=true, to_apply=%region_7.8 | all-reduce | flops 2 | bytes 16 | tf_op jit(solution)/shard_map/psum | solution.py:219
  306.6 73.7 %psum.52 = f32[]{:T(128)} all-reduce(f32[]{:T(128)} %multiply_reduce_fusion.2), channel_id=1, replica_groups=mesh['gx'=8,'gy'=32] {'gx','gy'}, use_global_device_ids=true, to_apply=%region_11.12 | all-reduce | flops 1 | bytes 8 | tf_op jit(solution)/shard_map/psum | solution.py:219
  389.8 4.0 collective-permute-start.14
  396.6 77.8 %psum.53 = f32[]{:T(128)} all-reduce(f32[]{:T(128)} %get-tuple-element.6), channel_id=1, replica_groups=mesh['gx'=8,'gy'=32] {'gx','gy'}, use_global_device_ids=true, to_apply=%region_13.14 | all-reduce | flops 1 | bytes 8 | tf_op jit(solution)/shard_map/psum | solution.py:226
  480.9 73.9 %psum.54 = f32[]{:T(128)} all-reduce(f32[]{:T(128)} %multiply_reduce_fusion), channel_id=1, replica_groups=mesh['gx'=8,'gy'=32] {'gx','gy'}, use_global_device_ids=true, to_apply=%region_15.16 | all-reduce | flops 1 | bytes 8 | tf_op jit(solution)/shard_map/psum | solution.py:219
  565.5 4.0 collective-permute-start.18
  571.5 77.2 %psum.55 = f32[]{:T(128)} all-reduce(f32[]{:T(128)} %fusion.26), channel_id=1, replica_groups=mesh['gx'=8,'gy'=32] {'gx','gy'}, use_global_device_ids=true, to_apply=%region_17.18 | all-reduce | flops 1 | bytes 8 | tf_op jit(solution)/shard_map/psum | solution.py:226
  (190 shorter events, 75.3 us)
Async XLA Ops:
  0.6 206.2 %copy-start = (f32[1,2,256,256]{3,2,1,0:T(8,128)S(1)}, f32[1,2,256,256]{3,2,1,0:T(8,128)}, u32[]{:S(2)}) copy-start(f32[1,2,256,256]{3,2,1,0:T(8,128)} %param.17) | copy-start | bytes 1572868
  10.0 8.0 %collective-permute-start.1 = (f32[3,1,32,256]{3,2,1,0:T(8,128)S(1)}, f32[3,1,32,256]{3,2,1,0:T(8,128)S(1)}, u32[]{:S(2)}, u32[]{:S(2)}) collective-permute-start(f32[3,1,32,256]{3,2,1,0:T(8,128)S(1)} %get-tuple-element.39), channel_id=1, source_target_pairs={{32,0},{64,32},{96,64},{128,96},{160,128},{192,160},{224,192},{33,... | collective-permute-start | bytes 294920 | tf_op jit(solution)/shard_map/ppermute | solution.py:25
  15.1 3.5 collective-permute-start
  18.7 5.5 collective-permute-start.3
  20.0 5.2 collective-permute-start.2
  31.9 87.3 %copy-start.41 = (f32[4]{0:T(128)S(1)}, f32[4]{0:T(128)}, u32[]{:S(2)}) copy-start(f32[4]{0:T(128)} %param.20) | copy-start | bytes 52
  168.2 29.8 %collective-permute-start.5 = (f32[1,32,256]{2,1,0:T(8,128)S(1)}, f32[1,32,256]{2,1,0:T(8,128)S(1)}, u32[]{:S(2)}, u32[]{:S(2)}) collective-permute-start(f32[1,32,256]{2,1,0:T(8,128)S(1)} %get-tuple-element.55), channel_id=1, source_target_pairs={{32,0},{64,32},{96,64},{128,96},{160,128},{192,160},{224,192},{33,... | collective-permute-start | bytes 98312 | tf_op jit(solution)/shard_map/ppermute | solution.py:25
  170.7 27.3 %collective-permute-start.4 = (f32[1,32,256]{2,1,0:T(8,128)S(1)}, f32[1,32,256]{2,1,0:T(8,128)S(1)}, u32[]{:S(2)}, u32[]{:S(2)}) collective-permute-start(f32[1,32,256]{2,1,0:T(8,128)S(1)} %get-tuple-element.54), channel_id=1, source_target_pairs={{0,32},{32,64},{64,96},{96,128},{128,160},{160,192},{192,224},{1,3... | collective-permute-start | bytes 98312 | tf_op jit(solution)/shard_map/ppermute | solution.py:22
  198.0 6.0 collective-permute-start.7
  199.3 5.2 collective-permute-start.6
  208.2 5.8 collective-permute-start.9
  210.1 4.7 collective-permute-start.8
  214.8 5.4 collective-permute-start.11
  216.1 4.9 collective-permute-start.10
  305.8 81.7 %copy-start.18 = (f32[16,32,255]{2,1,0:T(8,128)S(1)}, f32[16,32,255]{2,1,0:T(8,128)}, u32[]{:S(2)}) copy-start(f32[16,32,255]{2,1,0:T(8,128)} %get-tuple-element.12) | copy-start | bytes 1566724
  381.6 6.1 collective-permute-start.13
  384.3 4.1 collective-permute-start.12
  388.5 5.4 collective-permute-start.15
  389.8 4.9 collective-permute-start.14
  557.1 6.8 %collective-permute-start.17 = (f32[1,32,256]{2,1,0:T(8,128)S(1)}, f32[1,32,256]{2,1,0:T(8,128)S(1)}, u32[]{:S(2)}, u32[]{:S(2)}) collective-permute-start(f32[1,32,256]{2,1,0:T(8,128)S(1)} %get-tuple-element.49), channel_id=1, source_target_pairs={{32,0},{64,32},{96,64},{128,96},{160,128},{192,160},{224,192},{33,... | collective-permute-start | bytes 98312 | tf_op jit(solution)/shard_map/ppermute | solution.py:25
  559.7 4.3 collective-permute-start.16
  564.0 5.5 collective-permute-start.19
  565.5 4.9 collective-permute-start.18
  570.5 79.5 %copy-start.6 = (f32[16,32,256]{2,1,0:T(8,128)S(1)}, f32[16,32,256]{2,1,0:T(8,128)}, u32[]{:S(2)}) copy-start(f32[16,32,256]{2,1,0:T(8,128)} %param.16) | copy-start | bytes 1572868
  (38 other events, 325.3 us)
where the time goes:
time: 653 us; the launch traced here: 651 us
  blocking collectives  467 us (72%)
  other arithmetic  64.6 us (10%)
  starting transfers between devices  56.6 us (9%)
  local copies, waits for them, and re-layouts  44.7 us (7%)
  between operations  7.91 us (1%)
    psum x3, blocking collectives, residual_product(): lax.psum(jnp.sum(residual_now * precond_now), ('gx', 'gy'))  228 us
    psum x2, blocking collectives, per_device(): lax.psum(jnp.sum(direction * image_field), ('gx', 'gy'))  155 us
    psum x1, blocking collectives, per_device(): well_sums = lax.psum(own_sums, ('gx', 'gy'))  83.6 us
    ppermute x10, starting transfers between devices, extended(): lax.ppermute(lax.slice_in_dim(block, block.shape[dim] - width, None, axis...  35.2 us
    scatter-add x4, other arithmetic, spread(): flat_field.at[slot_index.reshape(-1)]  28.2 us
    gather x5, local copies, waits for them, and re-layouts, pick(): return field_values.reshape(-1)[slot_index]  27.8 us
    ppermute x10, starting transfers between devices, extended(): lax.ppermute(lax.slice_in_dim(block, 0, width, axis=dim), axis, backward)  21.4 us
  transfers between devices with their start and end apart: 20, of which 9 were waited for; matrix products, arithmetic and copies ran while one was open for 4% of the time, Pallas kernels for 0%

commit v1 on v0

v1 whole, which is shorter than its diff:
```python
import functools

import jax
import jax.numpy as jnp
from jax import lax
from jax.experimental import pallas as pl
from jax.experimental.pallas import tpu as pltpu
from jax.sharding import PartitionSpec as P

MESH = pl.DeviceIdType.MESH
HIGHEST = lax.Precision.HIGHEST
BLOCK = 16
BASIS = 3
RING = 8
TIME_STEP = 0.002
SHIFT = 1.0 / 16.0

SAT, PRS, PERM, TOTAL, BASE = 0, 1, 2, 3, 4
EXCHANGES = BASE + BASIS
LO_X, HI_X, LO_Y, HI_Y = 0, 1, 2, 3


def harmonic(former, latter):
    return 2.0 * former * latter / (former + latter)


def upwind(face, p_a, p_b, f_a, f_b):
    flow = face * (p_a - p_b)
    return flow * jnp.where(flow > 0.0, f_a, f_b)


def kernel(
    sizes,
    inj_cell,
    inj_rate,
    pro_cell,
    pro_pressure,
    perm_table,
    poro_table,
    inj_index,
    pro_index,
    rock_hbm,
    sat_hbm,
    prs_hbm,
    fac_hbm,
    satn_hbm,
    out_hbm,
    sat,
    prs,
    rock,
    fac,
    prod_hi,
    prod_lo,
    perm,
    dtp,
    poro,
    frac,
    mob,
    select,
    spots,
    face_x,
    face_y,
    face_z,
    low_x,
    side_y,
    div,
    well_d,
    well_e,
    satn,
    total,
    diag,
    resid,
    base,
    image,
    halo_x,
    halo_y,
    pack_y,
    own_z,
    slot_z,
    own_y,
    slot_y,
    own_a,
    slot_a,
    own_b,
    slot_b,
    load_sem,
    store_sem,
    face_send,
    face_recv,
    wz_send,
    wz_recv,
    wy_send,
    wy_recv,
    a_send,
    a_recv,
    b_send,
    b_recv,
):
    rows, cols, layers, n_gx, n_gy = sizes
    cells = rows * cols
    full_cols = cols * n_gy
    n_y = n_gy // RING
    plane = n_gx * n_y
    injectors = inj_index.shape[0]
    producers = pro_index.shape[0]
    perfs = inj_index.shape[1]

    gx = lax.axis_index("gx")
    gy = lax.axis_index("gy")
    yy = gy // RING
    zz = gy % RING
    spot_a = gx * n_y + yy

    def row(x):
        return pl.ds(pl.multiple_of(x * cols, cols), cols)

    def take(ref, c):
        parts = [ref[pl.ds(x * cols + c, 1), :] for x in range(rows)]
        return jnp.concatenate(parts, axis=0)

    def add_to(ref, c, value):
        for x in range(rows):
            ref[pl.ds(x * cols + c, 1), :] += value[x : x + 1]

    neighbours = (
        (lax.rem(gx + n_gx - 1, n_gx), gy),
        (lax.rem(gx + 1, n_gx), gy),
        (gx, lax.rem(gy + n_gy - 1, n_gy)),
        (gx, lax.rem(gy + 1, n_gy)),
    )

    def z_peer(p):
        return (gx, yy * RING + lax.rem(zz + p, RING))

    def plane_peer(p):
        spot = lax.rem(spot_a + p, plane)
        return (spot // n_y, lax.rem(spot, n_y) * RING + zz)

    def y_peer(p):
        return (gx, lax.rem(yy + p, n_y) * RING + zz)

    loads = [
        pltpu.make_async_copy(src, dst, load_sem.at[i])
        for i, (src, dst) in enumerate(
            ((sat_hbm, sat), (rock_hbm, rock), (prs_hbm, prs), (fac_hbm, fac))
        )
    ]
    for load in loads:
        load.start()

    barrier = pltpu.get_barrier_semaphore()
    for peer in neighbours:
        pl.semaphore_signal(barrier, inc=1, device_id=peer, device_id_type=MESH)

    @pl.loop(1, RING)
    def _(p):
        pl.semaphore_signal(barrier, inc=1, device_id=z_peer(p), device_id_type=MESH)

    @pl.loop(1, plane)
    def _(p):
        pl.semaphore_signal(barrier, inc=1, device_id=plane_peer(p), device_id_type=MESH)

    lane = lax.broadcasted_iota(jnp.int32, (1, 128), 1)
    well_row = jnp.full((1, 128), -1, jnp.int32)
    well_layer = jnp.full((1, 128), -1, jnp.int32)
    pressure_row = jnp.zeros((1, 128), jnp.float32)
    rate_row = jnp.zeros((1, 128), jnp.float32)
    spread = lax.broadcasted_iota(jnp.int32, (cols, perfs), 0) - lax.broadcasted_iota(
        jnp.int32, (cols, perfs), 1
    )
    lane_wide = lax.broadcasted_iota(jnp.int32, (cols, 128), 1)
    column = jnp.zeros((cols, 128), jnp.float32)
    for w in range(producers + injectors):
        produces = w < producers
        cell_ref = pro_cell if produces else inj_cell
        index_ref = pro_index if produces else inj_index
        i = w if produces else w - producers
        cell = cell_ref[i, 0, 0]
        well_row = jnp.where(lane == w, cell // full_cols - gx * rows, well_row)
        well_layer = jnp.where(lane == w, cell_ref[i, 1, 0], well_layer)
        start = cell % full_cols
        offset = spread + (gy * cols - start)
        hit = jnp.where(
            (offset == 0) | (offset == full_cols) | (offset == -full_cols),
            index_ref[i : i + 1, :],
            0.0,
        )
        column = jnp.where(lane_wide == w, jnp.sum(hit, axis=1, keepdims=True), column)
        if produces:
            pressure_row = jnp.where(lane == w, pro_pressure[i], pressure_row)
        else:
            rate_row = jnp.where(lane == w, inj_rate[i], rate_row)
    is_producer = jnp.where(lane < producers, 1.0, 0.0)
    layer_pos = lax.broadcasted_iota(jnp.int32, (layers, 128), 0)
    spots[...] = jnp.where(layer_pos == well_layer, 1.0, 0.0)

    @pl.loop(0, rows)
    def _(x):
        select[row(x), :] = jnp.where(well_row == x, column, 0.0)

    loads[0].wait()

    @pl.loop(0, rows)
    def _(x):
        s = sat[row(x), :]
        water = 2.0 * s * s
        rest = 1.0 - s
        t = water + rest * rest
        mob[row(x), :] = t
        frac[row(x), :] = water / t

    picked = jnp.dot(
        mob[...], spots[...], precision=HIGHEST, preferred_element_type=jnp.float32
    )
    own_z[0] = jnp.sum(picked * select[...], axis=0, keepdims=True)

    loads[1].wait()

    @pl.loop(0, rows)
    def _(x):
        kind = rock[row(x), :]
        bit0 = (kind & 1) == 1
        bit1 = (kind & 2) == 2
        bit2 = kind >= 4

        def lookup(table):
            pairs = [jnp.where(bit0, table[2 * i + 1], table[2 * i]) for i in range(4)]
            return jnp.where(
                bit2, jnp.where(bit1, pairs[3], pairs[2]), jnp.where(bit1, pairs[1], pairs[0])
            )

        perm[row(x), :] = lookup(perm_table)
        porosity = lookup(poro_table)
        poro[row(x), :] = porosity
        dtp[row(x), :] = TIME_STEP / porosity

    loads[2].wait()
    for e, field in ((SAT, sat), (PRS, prs), (PERM, perm)):
        pack_y[e, 0] = take(field, 0)
        pack_y[e, 1] = take(field, cols - 1)

    def face_copy(e, d):
        field = (sat, prs, perm, total)[e] if e < BASE else base.at[e - BASE]
        if d == LO_X:
            src, dst = field.at[pl.ds(0, cols), :], halo_x.at[e, 1]
        elif d == HI_X:
            src, dst = field.at[pl.ds(cells - cols, cols), :], halo_x.at[e, 0]
        elif d == LO_Y:
            src, dst = pack_y.at[e, 0], halo_y.at[e, 1]
        else:
            src, dst = pack_y.at[e, 1], halo_y.at[e, 0]
        return pltpu.make_async_remote_copy(
            src_ref=src,
            dst_ref=dst,
            send_sem=face_send.at[e, d],
            recv_sem=face_recv.at[e, d],
            device_id=neighbours[d],
            device_id_type=MESH,
        )

    def send_faces(e):
        for d in range(4):
            face_copy(e, d).start()

    def take_faces(e):
        for d in range(4):
            face_copy(e, d).wait_recv()

    def z_copy(p, own, slots, send, recv):
        return pltpu.make_async_remote_copy(
            src_ref=own.at[0],
            dst_ref=slots.at[p],
            send_sem=send.at[p],
            recv_sem=recv.at[p],
            device_id=z_peer(p),
            device_id_type=MESH,
        )

    def plane_copy(p):
        return pltpu.make_async_remote_copy(
            src_ref=own_a.at[0],
            dst_ref=slot_a.at[p],
            send_sem=a_send.at[p],
            recv_sem=a_recv.at[p],
            device_id=plane_peer(p),
            device_id_type=MESH,
        )

    def y_copy(i):
        return pltpu.make_async_remote_copy(
            src_ref=own_y.at[0],
            dst_ref=slot_y.at[i],
            send_sem=wy_send.at[i],
            recv_sem=wy_recv.at[i],
            device_id=y_peer(1 if i == 0 else n_y - 1),
            device_id_type=MESH,
        )

    pl.semaphore_wait(barrier, 4 + (RING - 1) + (plane - 1))

    @pl.loop(1, RING)
    def _(p):
        z_copy(p, own_z, slot_z, wz_send, wz_recv).start()

    for e in (SAT, PRS, PERM):
        send_faces(e)

    lane_z = lax.broadcasted_iota(jnp.int32, (cols, layers), 1)
    col_y = lax.broadcasted_iota(jnp.int32, (cols, layers), 0)
    inner_z = lane_z < layers - 1
    inner_y = col_y < cols - 1

    def next_y(v):
        return pltpu.roll(v, cols - 1, 0)

    def last_y(v):
        return pltpu.roll(v, 1, 0)

    def next_z(v):
        return pltpu.roll(v, layers - 1, 1)

    def last_z(v):
        return pltpu.roll(v, 1, 1)

    well_d[...] = lax.dot_general(
        select[...],
        spots[...] * is_producer,
        (((1,), (1,)), ((), ())),
        precision=HIGHEST,
        preferred_element_type=jnp.float32,
    )
    well_e[...] = lax.dot_general(
        select[...],
        spots[...] * pressure_row,
        (((1,), (1,)), ((), ())),
        precision=HIGHEST,
        preferred_element_type=jnp.float32,
    )

    zero_row = jnp.zeros((cols, layers), jnp.float32)

    def flux_row(x, flux_last):
        here, there = row(x), row(jnp.minimum(x + 1, rows - 1))
        k, p, f = perm[here, :], prs[here, :], frac[here, :]
        kx, px, fx = perm[there, :], prs[there, :], frac[there, :]
        tx = harmonic(k, kx)
        ty = jnp.where(inner_y, harmonic(k, next_y(k)), 0.0)
        tz = jnp.where(inner_z, 0.1 * harmonic(k, next_z(k)), 0.0)
        face_x[here, :] = tx
        face_y[here, :] = ty
        face_z[here, :] = tz
        wx = upwind(tx, p, px, f, fx)
        wy = upwind(ty, p, next_y(p), f, next_y(f))
        wz = upwind(tz, p, next_z(p), f, next_z(f))
        s = sat[here, :]
        made = 2.0 * s * s * (p * well_d[here, :] - well_e[here, :])
        div[here, :] = (
            made + (wx - flux_last) + (wy - last_y(wy)) + (wz - last_z(wz))
        )
        return wx

    lax.fori_loop(0, rows, flux_row, zero_row)

    loads[3].wait()
    for b in range(cols // BLOCK):
        lower = fac[b]
        gram = lax.dot_general(
            lower,
            lower,
            (((0,), (0,)), ((), ())),
            precision=HIGHEST,
            preferred_element_type=jnp.float32,
        )
        high = gram.astype(jnp.bfloat16)
        prod_hi[b] = high
        prod_lo[b] = (gram - high.astype(jnp.float32)).astype(jnp.bfloat16)

    @pl.loop(1, RING)
    def _(p):
        z_copy(p, own_z, slot_z, wz_send, wz_recv).wait_recv()

    slot_z[0] = own_z[0]
    own_y[0] = jnp.sum(slot_z[...], axis=0)
    for i in range(2):
        y_copy(i).start()

    for e in (SAT, PRS, PERM):
        take_faces(e)

    def fraction(s):
        water = 2.0 * s * s
        rest = 1.0 - s
        return water / (water + rest * rest)

    inner_low_x = jnp.where(gx > 0, 1.0, 0.0)
    inner_high_x = jnp.where(gx < n_gx - 1, 1.0, 0.0)
    inner_low_y = jnp.where(gy > 0, 1.0, 0.0)
    inner_high_y = jnp.where(gy < n_gy - 1, 1.0, 0.0)
    first, final = pl.ds(0, cols), pl.ds(cells - cols, cols)

    t = inner_low_x * harmonic(halo_x[PERM, 0], perm[first, :])
    low_x[...] = t
    div[first, :] -= upwind(
        t, halo_x[PRS, 0], prs[first, :], fraction(halo_x[SAT, 0]), frac[first, :]
    )
    t = inner_high_x * harmonic(perm[final, :], halo_x[PERM, 1])
    face_x[final, :] = t
    div[final, :] += upwind(
        t, prs[final, :], halo_x[PRS, 1], frac[final, :], fraction(halo_x[SAT, 1])
    )
    t = inner_low_y * harmonic(halo_y[PERM, 0], pack_y[PERM, 0])
    side_y[0] = t
    flux = upwind(
        t, halo_y[PRS, 0], pack_y[PRS, 0], fraction(halo_y[SAT, 0]), fraction(pack_y[SAT, 0])
    )
    add_to(div, 0, -flux)
    t = inner_high_y * harmonic(pack_y[PERM, 1], halo_y[PERM, 1])
    side_y[1] = t
    flux = upwind(
        t, pack_y[PRS, 1], halo_y[PRS, 1], fraction(pack_y[SAT, 1]), fraction(halo_y[SAT, 1])
    )
    add_to(div, cols - 1, flux)

    for i in range(2):
        y_copy(i).wait_recv()
    sums = own_y[0] + slot_y[0] + slot_y[1]
    scale = jnp.where(sums > 0.0, rate_row / jnp.where(sums > 0.0, sums, 1.0), 0.0)
    diag[...] = lax.dot_general(
        select[...],
        spots[...] * scale,
        (((1,), (1,)), ((), ())),
        precision=HIGHEST,
        preferred_element_type=jnp.float32,
    )

    @pl.loop(0, rows)
    def _(x):
        here = row(x)
        source = mob[here, :] * diag[here, :]
        s = sat[here, :] - dtp[here, :] * (div[here, :] - source)
        satn[here, :] = s
        resid[here, :] = source
        rest = 1.0 - s
        total[here, :] = 2.0 * s * s + rest * rest

    pack_y[TOTAL, 0] = take(total, 0)
    pack_y[TOTAL, 1] = take(total, cols - 1)
    send_faces(TOTAL)
    store_satn = pltpu.make_async_copy(satn, satn_hbm, store_sem.at[0])
    store_satn.start()

    def residual_row(x, flux_last):
        here, there = row(x), row(jnp.minimum(x + 1, rows - 1))
        t, tx = total[here, :], total[there, :]
        p, px = prs[here, :], prs[there, :]
        cx = face_x[here, :] * (0.5 * (t + tx))
        cy = face_y[here, :] * (0.5 * (t + next_y(t)))
        cz = face_z[here, :] * (0.5 * (t + next_z(t)))

        @pl.when(x < rows - 1)
        def _():
            face_x[here, :] = cx

        face_y[here, :] = cy
        face_z[here, :] = cz
        d, e = well_d[here, :], well_e[here, :]
        diag[here, :] = poro[here, :] + d * t
        fx = cx * (p - px)
        fy = cy * (p - next_y(p))
        fz = cz * (p - next_z(p))
        resid[here, :] = (
            resid[here, :]
            + t * (e - d * p)
            - ((fx - flux_last) + (fy - last_y(fy)) + (fz - last_z(fz)))
        )
        return fx

    lax.fori_loop(0, rows, residual_row, zero_row)

    take_faces(TOTAL)
    c = low_x[...] * (0.5 * (total[first, :] + halo_x[TOTAL, 0]))
    low_x[...] = c
    resid[first, :] -= c * (prs[first, :] - halo_x[PRS, 0])
    c = face_x[final, :] * (0.5 * (total[final, :] + halo_x[TOTAL, 1]))
    face_x[final, :] = c
    resid[final, :] -= c * (prs[final, :] - halo_x[PRS, 1])
    for i, at in ((0, 0), (1, cols - 1)):
        c = side_y[i] * (0.5 * (pack_y[TOTAL, i] + halo_y[TOTAL, i]))
        side_y[i] = c
        add_to(resid, at, -c * (pack_y[PRS, i] - halo_y[PRS, i]))

    def precondition(src, dst, factor):
        for b in range(cols // BLOCK):
            parts = [
                src[pl.ds(x * cols + b * BLOCK, BLOCK), :] for x in range(rows)
            ]
            v = jnp.concatenate(parts, axis=0)
            if factor is not None:
                v = v * factor
            high = v.astype(jnp.bfloat16)
            low = (v - high.astype(jnp.float32)).astype(jnp.bfloat16)
            z = jnp.dot(high, prod_hi[b], preferred_element_type=jnp.float32)
            z += jnp.dot(high, prod_lo[b], preferred_element_type=jnp.float32)
            z += jnp.dot(low, prod_hi[b], preferred_element_type=jnp.float32)
            for x in range(rows):
                dst[pl.ds(x * cols + b * BLOCK, BLOCK), :] = z[x * BLOCK : (x + 1) * BLOCK]

    for k in range(BASIS):
        e = BASE + k
        vec, img = base.at[k], image.at[k]
        precondition(resid if k == 0 else image.at[k - 1], vec, None if k == 0 else SHIFT)
        pack_y[e, 0] = take(vec, 0)
        pack_y[e, 1] = take(vec, cols - 1)
        send_faces(e)

        def image_row(x, flux_last, vec=vec, img=img):
            here, there = row(x), row(jnp.minimum(x + 1, rows - 1))
            v, vx = vec[here, :], vec[there, :]
            fx = face_x[here, :] * (v - vx)
            fy = face_y[here, :] * (v - next_y(v))
            fz = face_z[here, :] * (v - next_z(v))
            img[here, :] = (
                diag[here, :] * v
                + (fx - flux_last)
                + (fy - last_y(fy))
                + (fz - last_z(fz))
            )
            return fx

        lax.fori_loop(0, rows, image_row, zero_row)
        take_faces(e)
        img[first, :] += low_x[...] * (vec[first, :] - halo_x[e, 0])
        img[final, :] += face_x[final, :] * (vec[final, :] - halo_x[e, 1])
        for i, at in ((0, 0), (1, cols - 1)):
            add_to(img, at, side_y[i] * (pack_y[e, i] - halo_y[e, i]))

    pairs = [(0, 0), (1, 0), (1, 1), (2, 0), (2, 1), (2, 2)]

    def dots_row(x, sums):
        here = row(x)
        v = [base[k, here, :] for k in range(BASIS)]
        u = [image[k, here, :] for k in range(BASIS)]
        r = resid[here, :]
        terms = [v[i] * u[j] for i, j in pairs] + [v[i] * r for i in range(BASIS)]
        out = []
        for s, term in zip(sums, terms):
            for i in range(cols // 8):
                s = s + term[8 * i : 8 * i + 8]
            out.append(s)
        return tuple(out)

    zero_sum = jnp.zeros((8, layers), jnp.float32)
    count = len(pairs) + BASIS
    sums = lax.fori_loop(0, rows, dots_row, (zero_sum,) * count)
    message = jnp.zeros((1, 128), jnp.float32)
    for i, s in enumerate(sums):
        s = jnp.sum(s, axis=0, keepdims=True)
        message = jnp.where(lane == i, jnp.sum(s, axis=1, keepdims=True), message)
    own_a[0] = message

    @pl.loop(1, plane)
    def _(p):
        plane_copy(p).start()

    @pl.loop(1, plane)
    def _(p):
        plane_copy(p).wait_recv()

    slot_a[0] = message
    own_b[0] = jnp.sum(slot_a[...], axis=0)

    @pl.loop(1, RING)
    def _(p):
        z_copy(p, own_b, slot_b, b_send, b_recv).start()

    @pl.loop(1, RING)
    def _(p):
        z_copy(p, own_b, slot_b, b_send, b_recv).wait_recv()

    slot_b[0] = own_b[0]
    result = jnp.sum(slot_b[...], axis=0)
    val = [result[:, i : i + 1] for i in range(count)]
    g00, g10, g11, g20, g21, g22, b0, b1, b2 = val

    def ratio(a, b):
        good = b > 0.0
        return jnp.where(good, a / jnp.where(good, b, 1.0), 0.0)

    l10, l20 = ratio(g10, g00), ratio(g20, g00)
    d1 = g11 - l10 * g10
    e21 = g21 - l20 * g10
    l21 = ratio(e21, d1)
    d2 = g22 - l20 * g20 - l21 * e21
    y1 = b1 - l10 * b0
    y2 = b2 - l20 * b0 - l21 * y1
    c2 = ratio(y2, d2)
    c1 = ratio(y1, d1) - l21 * c2
    c0 = ratio(b0, g00) - l10 * c1 - l20 * c2

    @pl.loop(0, rows)
    def _(x):
        here = row(x)
        div[here, :] = prs[here, :] + (
            c0 * base[0, here, :] + c1 * base[1, here, :] + c2 * base[2, here, :]
        )

    store_out = pltpu.make_async_copy(div, out_hbm, store_sem.at[1])
    store_out.start()

    @pl.loop(1, RING)
    def _(p):
        z_copy(p, own_z, slot_z, wz_send, wz_recv).wait_send()
        z_copy(p, own_b, slot_b, b_send, b_recv).wait_send()

    @pl.loop(1, plane)
    def _(p):
        plane_copy(p).wait_send()

    for i in range(2):
        y_copy(i).wait_send()
    for e in range(EXCHANGES):
        for d in range(4):
            face_copy(e, d).wait_send()
    store_satn.wait()
    store_out.wait()


def solution(mesh):
    n_gx, n_gy = mesh.shape["gx"], mesh.shape["gy"]

    def per_device(
        rock_type,
        perm_table,
        poro_table,
        saturation,
        pressure_old,
        factor_inverse,
        inject_cells,
        inject_index,
        inject_rate,
        produce_cells,
        produce_index,
        produce_pressure,
    ):
        rows, cols, layers = saturation.shape
        cells = rows * cols
        blocks = cols // BLOCK
        f32, bf16 = jnp.float32, jnp.bfloat16
        flat = (cells, layers)
        field = pltpu.VMEM(flat, f32)
        smem = pl.BlockSpec(memory_space=pltpu.SMEM)
        vmem = pl.BlockSpec(memory_space=pltpu.VMEM)
        hbm = pl.BlockSpec(memory_space=pl.ANY)
        plane = n_gx * (n_gy // RING)
        dma = pltpu.SemaphoreType.DMA
        scratch = [
            field,
            field,
            pltpu.VMEM(flat, jnp.int32),
            pltpu.VMEM((blocks, layers, layers), f32),
            pltpu.VMEM((blocks, layers, layers), bf16),
            pltpu.VMEM((blocks, layers, layers), bf16),
            field,
            field,
            field,
            field,
            field,
            pltpu.VMEM((cells, 128), f32),
            pltpu.VMEM((layers, 128), f32),
            field,
            field,
            field,
            pltpu.VMEM((cols, layers), f32),
            pltpu.VMEM((2, rows, layers), f32),
            field,
            field,
            field,
            field,
            field,
            field,
            field,
            pltpu.VMEM((BASIS,) + flat, f32),
            pltpu.VMEM((BASIS,) + flat, f32),
            pltpu.VMEM((EXCHANGES, 2, cols, layers), f32),
            pltpu.VMEM((EXCHANGES, 2, rows, layers), f32),
            pltpu.VMEM((EXCHANGES, 2, rows, layers), f32),
            pltpu.VMEM((1, 1, 128), f32),
            pltpu.VMEM((RING, 1, 128), f32),
            pltpu.VMEM((1, 1, 128), f32),
            pltpu.VMEM((2, 1, 128), f32),
            pltpu.VMEM((1, 1, 128), f32),
            pltpu.VMEM((plane, 1, 128), f32),
            pltpu.VMEM((1, 1, 128), f32),
            pltpu.VMEM((RING, 1, 128), f32),
            dma((4,)),
            dma((2,)),
            dma((EXCHANGES, 4)),
            dma((EXCHANGES, 4)),
            dma((RING,)),
            dma((RING,)),
            dma((2,)),
            dma((2,)),
            dma((plane,)),
            dma((plane,)),
            dma((RING,)),
            dma((RING,)),
        ]
        satn, out = pl.pallas_call(
            functools.partial(kernel, (rows, cols, layers, n_gx, n_gy)),
            out_shape=[jax.ShapeDtypeStruct(flat, f32)] * 2,
            in_specs=[smem] * 6 + [vmem] * 2 + [hbm] * 4,
            out_specs=[hbm] * 2,
            scratch_shapes=scratch,
            compiler_params=pltpu.CompilerParams(
                collective_id=0, has_side_effects=True, vmem_limit_bytes=60 * 1024 * 1024
            ),
            name="reservoir_step",
        )(
            jnp.swapaxes(inject_cells, 1, 2),
            inject_rate,
            jnp.swapaxes(produce_cells, 1, 2),
            produce_pressure,
            perm_table,
            poro_table,
            inject_index,
            produce_index,
            rock_type.reshape(flat),
            saturation.reshape(flat),
            pressure_old.reshape(flat),
            factor_inverse.reshape(blocks, layers, layers),
        )
        return satn.reshape(saturation.shape), out.reshape(saturation.shape)

    grid = P("gx", "gy", None)
    in_specs = (grid, P(), P(), grid, grid, P("gx", "gy", None, None)) + (P(),) * 6
    return jax.shard_map(
        per_device, mesh=mesh, in_specs=in_specs, out_specs=(grid, grid), check_vma=False
    )
```

time: 653 us -> 55.2 us (0.08)
  blocking collectives: 467 us -> 0 us
  other arithmetic: 64.6 us -> 0 us
  starting transfers between devices: 56.6 us -> 0 us
  Pallas kernels: 0 us -> 51.7 us
  local copies, waits for them, and re-layouts: 44.7 us -> 2.74 us
  between operations: 7.91 us -> 0.65 us
    psum x6 -> x0, blocking collectives: 467 us -> none  [the longest x3 228 us: residual_product(): lax.psum(jnp.sum(residual_now * precond_now), ('gx', 'gy'))]
    ppermute x20 -> x0, starting transfers between devices: 56.6 us -> none  [the longest x10 35.2 us: extended(): lax.ppermute(lax.slice_in_dim(block, block.shape[dim] - width, None, axis...]
    pallas_call x0 -> x1, Pallas kernels: none -> 51.7 us  [per_device(): pl.pallas_call(functools.partial(kernel, (rows, cols, layers, n_gx, n_gy)...]
    scatter-add x4 -> x0, other arithmetic: 28.2 us -> none  [spread(): flat_field.at[slot_index.reshape(-1)]]
    gather x5 -> x0, local copies, waits for them, and re-layouts: 27.8 us -> none  [pick(): return field_values.reshape(-1)[slot_index]]
    add x4 -> x0, other arithmetic: 10.2 us -> none  [the longest x1 8 us: total_mobility(): saturation * saturation / water_viscosity]
    mul x16 -> x0, other arithmetic: 8.21 us -> none  [the longest x4 3.11 us: apply_padded(): across_z = coef_z * (vector[:, :, :-1] - vector[:, :, 1:])]
    another operation x1 -> x0, other arithmetic: 7.66 us -> none  [per_device(): jnp.stack([saturation, pressure_old, permeability])]
  transfers between devices with their start and end apart: 20 -> 0, of which waited for: 9 -> 0; matrix products, arithmetic and copies ran while one was open for 4% -> 0% of each run, Pallas kernels for 0% -> 0%
where the time goes in v1:
time: 55.2 us; the launch traced here: 55 us
  Pallas kernels  51.7 us (94%)
  local copies, waits for them, and re-layouts  2.74 us (5%)
  between operations  0.65 us (1%)
    pallas_call x1, Pallas kernels, per_device(): pl.pallas_call(functools.partial(kernel, (rows, cols, layers, n_gx, n_gy)...  51.7 us
    unnamed x4, local copies, waits for them, and re-layouts  2.74 us

profile of v1, /device:TPU:1, one launch (start us, length us, event | category | flops | bytes accessed | tf_op | source)
XLA Modules:
  0.0 55.0 jit_solution(14956677628077861550)
XLA Ops:
  0.6 51.7 %reservoir_step.1 = (f32[512,256]{1,0:T(8,128)}, f32[512,256]{1,0:T(8,128)}) custom-call(s32[4,2,128]{2,1,0:T(2,128)} %bitcast.15, f32[4]{0:T(128)} %inj_rate.1, s32[8,2,128]{2,1,0:T(2,128)} %bitcast.14, f32[8]{0:T(128)} %pro_pressure.1, f32[8]{0:T(128)} %perm_table.1, f32[8]{0:T(128)} %poro_table.1, f32[4,128]{1,0:T(4,128)} %inj_index.1, ...), custom_call_target="tpu_custom_call" | custom-call | tf_op jit(solution)/shard_map/reservoir_step/pallas_call | solution.py:708
  52.3 0.0 copy-start
  52.3 1.9 %copy.16 = f32[16,32,256]{2,1,0:T(8,128)} copy(f32[16,32,256]{2,1,0:T(8,128)} %bitcast.9) | data formatting | bytes 1048576
  54.2 0.0 copy-done
  54.2 0.8 %copy.17 = f32[16,32,256]{2,1,0:T(8,128)} copy(f32[16,32,256]{2,1,0:T(8,128)S(1)} %bitcast.8) | data formatting | bytes 1048576
Async XLA Ops:
  52.3 2.0 %copy-start = (f32[512,256]{1,0:T(8,128)S(1)}, f32[512,256]{1,0:T(8,128)}, u32[]{:S(2)}) copy-start(f32[512,256]{1,0:T(8,128)} %get-tuple-element.5) | copy-start | bytes 1572868

commit v2 on v1

v2 whole, which is shorter than its diff:
```python
import functools

import jax
import jax.numpy as jnp
from jax import lax
from jax.experimental import pallas as pl
from jax.experimental.pallas import tpu as pltpu
from jax.sharding import PartitionSpec as P

MESH = pl.DeviceIdType.MESH
HIGHEST = lax.Precision.HIGHEST
BLOCK = 16
BASIS = 3
RING = 8
TIME_STEP = 0.002
SHIFT = 2.0**-14

INPUT, MOVED, BASE = 0, 1, 2
EXCHANGES = BASE + BASIS
SAT, PRS, PERM, DTP = 0, 1, 2, 3
LO_X, HI_X, LO_Y, HI_Y = 0, 1, 2, 3
REACH_X, REACH_Y = 1, 5


def harmonic(former, latter):
    return 2.0 * former * latter / (former + latter)


def upwind(face, p_a, p_b, f_a, f_b):
    flow = face * (p_a - p_b)
    return flow * jnp.where(flow > 0.0, f_a, f_b)


def kernel(
    sizes,
    inj_cell,
    inj_rate,
    pro_cell,
    pro_pressure,
    perm_table,
    poro_table,
    inj_index,
    pro_index,
    rock_hbm,
    sat_hbm,
    prs_hbm,
    fac_hbm,
    made_hbm,
    coef_out,
    inp,
    rock,
    fac,
    prod_hi,
    prod_lo,
    poro,
    frac,
    mob,
    select,
    spots,
    face_x,
    face_y,
    face_z,
    low_x,
    side_y,
    moved,
    well_d,
    well_e,
    source,
    satn,
    total,
    diag,
    resid,
    base,
    image,
    input_x,
    input_y,
    input_pack,
    halo_x,
    halo_y,
    pack_y,
    own,
    slot_w,
    slot_a,
    slot_b,
    load_sem,
    store_sem,
    face_send,
    face_recv,
    group_send,
    group_recv,
):
    rows, cols, layers, n_gx, n_gy = sizes
    cells = rows * cols
    full_cols = cols * n_gy
    n_y = n_gy // RING
    plane = n_gx * n_y
    injectors = inj_index.shape[0]
    producers = pro_index.shape[0]
    perfs = inj_index.shape[1]
    sat, prs, perm, dtp = (inp.at[i] for i in range(4))

    gx = lax.axis_index("gx")
    gy = lax.axis_index("gy")
    yy = gy // RING
    zz = gy % RING
    spot_a = gx * n_y + yy

    def row(x):
        return pl.ds(pl.multiple_of(x * cols, cols), cols)

    def take(ref, c):
        parts = [ref[pl.ds(x * cols + c, 1), :] for x in range(rows)]
        return jnp.concatenate(parts, axis=0)

    def add_to(ref, c, value):
        for x in range(rows):
            ref[pl.ds(x * cols + c, 1), :] += value[x : x + 1]

    neighbours = (
        (lax.rem(gx + n_gx - 1, n_gx), gy),
        (lax.rem(gx + 1, n_gx), gy),
        (gx, lax.rem(gy + n_gy - 1, n_gy)),
        (gx, lax.rem(gy + 1, n_gy)),
    )
    sends = (gx > 0, gx < n_gx - 1, gy > 0, gy < n_gy - 1)
    hears = (gx < n_gx - 1, gx > 0, gy < n_gy - 1, gy > 0)

    def z_peer(p):
        return (gx, yy * RING + lax.rem(zz + p, RING))

    def plane_peer(p):
        spot = lax.rem(spot_a + p, plane)
        return (spot // n_y, lax.rem(spot, n_y) * RING + zz)

    width = 2 * REACH_Y + 1
    window = (2 * REACH_X + 1) * width
    centre = window // 2

    def window_peer(q):
        return (
            lax.rem(gx + n_gx - REACH_X + q // width, n_gx),
            lax.rem(gy + n_gy - REACH_Y + lax.rem(q, width), n_gy),
        )

    def window_each(action):
        pl.loop(0, centre)(lambda q: action(q, q))
        pl.loop(centre + 1, window)(lambda q: action(q, q - 1))

    loads = [
        pltpu.make_async_copy(src, dst, load_sem.at[i])
        for i, (src, dst) in enumerate(
            ((sat_hbm, sat), (rock_hbm, rock), (prs_hbm, prs), (fac_hbm, fac))
        )
    ]
    for load in loads:
        load.start()

    barrier = pltpu.get_barrier_semaphore()

    def greet(peer):
        pl.semaphore_signal(barrier, inc=1, device_id=peer, device_id_type=MESH)

    window_each(lambda q, slot: greet(window_peer(q)))
    pl.loop(1, RING)(lambda p: greet(z_peer(p)))
    pl.loop(1, plane)(lambda p: greet(plane_peer(p)))

    def clear_x(at):
        input_x[at] = jnp.zeros(input_x.shape[1:], jnp.float32)
        for e in range(EXCHANGES - 1):
            halo_x[e, at] = jnp.zeros(halo_x.shape[2:], jnp.float32)

    def clear_y(at):
        input_y[at] = jnp.zeros(input_y.shape[1:], jnp.float32)
        for e in range(EXCHANGES - 1):
            halo_y[e, at] = jnp.zeros(halo_y.shape[2:], jnp.float32)

    pl.when(gx == 0)(lambda: clear_x(0))
    pl.when(gx == n_gx - 1)(lambda: clear_x(1))
    pl.when(gy == 0)(lambda: clear_y(0))
    pl.when(gy == n_gy - 1)(lambda: clear_y(1))

    lane = lax.broadcasted_iota(jnp.int32, (1, 128), 1)
    well_row = jnp.full((1, 128), -9, jnp.int32)
    well_layer = jnp.full((1, 128), -9, jnp.int32)
    pressure_row = jnp.zeros((1, 128), jnp.float32)
    rate_row = jnp.zeros((1, 128), jnp.float32)
    wide = cols + 16
    spread = lax.broadcasted_iota(jnp.int32, (wide, perfs), 0) - lax.broadcasted_iota(
        jnp.int32, (wide, perfs), 1
    )
    lane_wide = lax.broadcasted_iota(jnp.int32, (wide, 128), 1)
    column = jnp.zeros((wide, 128), jnp.float32)
    for w in range(producers + injectors):
        produces = w < producers
        cell_ref = pro_cell if produces else inj_cell
        index_ref = pro_index if produces else inj_index
        i = w if produces else w - producers
        cell = cell_ref[i, 0, 0]
        well_row = jnp.where(lane == w, cell // full_cols - gx * rows, well_row)
        well_layer = jnp.where(lane == w, cell_ref[i, 1, 0], well_layer)
        start = cell % full_cols
        offset = spread + (gy * cols - 8 - start)
        hit = jnp.where(
            (offset == 0) | (offset == full_cols) | (offset == -full_cols),
            index_ref[i : i + 1, :],
            0.0,
        )
        column = jnp.where(lane_wide == w, jnp.sum(hit, axis=1, keepdims=True), column)
        if produces:
            pressure_row = jnp.where(lane == w, pro_pressure[i], pressure_row)
        else:
            rate_row = jnp.where(lane == w, inj_rate[i], rate_row)
    is_producer = jnp.where(lane < producers, 1.0, 0.0)
    layer_pos = lax.broadcasted_iota(jnp.int32, (layers, 128), 0)
    spots[...] = jnp.where(layer_pos == well_layer, 1.0, 0.0)
    own_column = column[8 : 8 + cols]
    for x in range(rows):
        select[x * cols : (x + 1) * cols, :] = jnp.where(well_row == x, own_column, 0.0)
    select[cells : cells + cols, :] = jnp.where(well_row == -1, own_column, 0.0)
    select[cells + cols : cells + 2 * cols, :] = jnp.where(well_row == rows, own_column, 0.0)
    row_pos = lax.broadcasted_iota(jnp.int32, (rows, 128), 0)
    rim_y = cells + 2 * cols
    select[rim_y : rim_y + rows, :] = jnp.where(row_pos == well_row, column[7:8], 0.0)
    select[rim_y + rows : rim_y + 2 * rows, :] = jnp.where(
        row_pos == well_row, column[8 + cols : 9 + cols], 0.0
    )

    loads[0].wait()

    def mobility(s):
        water = 2.0 * s * s
        rest = 1.0 - s
        return water, water + rest * rest

    @pl.loop(0, rows)
    def _(x):
        water, t = mobility(sat[row(x), :])
        mob[row(x), :] = t
        frac[row(x), :] = water / t

    picked = jnp.dot(
        mob[...], spots[...], precision=HIGHEST, preferred_element_type=jnp.float32
    )
    own[0] = jnp.sum(picked * select[pl.ds(0, cells), :], axis=0, keepdims=True)

    loads[1].wait()

    @pl.loop(0, rows)
    def _(x):
        kind = rock[row(x), :]
        bit0 = (kind & 1) == 1
        bit1 = (kind & 2) == 2
        bit2 = kind >= 4

        def lookup(table):
            pairs = [jnp.where(bit0, table[2 * i + 1], table[2 * i]) for i in range(4)]
            return jnp.where(
                bit2, jnp.where(bit1, pairs[3], pairs[2]), jnp.where(bit1, pairs[1], pairs[0])
            )

        perm[row(x), :] = lookup(perm_table)
        porosity = lookup(poro_table)
        poro[row(x), :] = porosity
        dtp[row(x), :] = TIME_STEP / porosity

    loads[2].wait()
    for i in range(4):
        input_pack[0, i] = take(inp.at[i], 0)
        input_pack[1, i] = take(inp.at[i], cols - 1)

    def face_copy(e, d):
        if e == INPUT:
            if d < 2:
                src = inp.at[:, pl.ds(0 if d == LO_X else cells - cols, cols), :]
                dst = input_x.at[1 - d]
            else:
                src, dst = input_pack.at[d - 2], input_y.at[3 - d]
        else:
            field = moved if e == MOVED else base.at[e - BASE]
            if d < 2:
                src = field.at[pl.ds(0 if d == LO_X else cells - cols, cols), :]
                dst = halo_x.at[e - 1, 1 - d]
            else:
                src, dst = pack_y.at[e - 1, d - 2], halo_y.at[e - 1, 3 - d]
        return pltpu.make_async_remote_copy(
            src_ref=src,
            dst_ref=dst,
            send_sem=face_send.at[d],
            recv_sem=face_recv.at[e % 2, d],
            device_id=neighbours[d],
            device_id_type=MESH,
        )

    def send_faces(e):
        for d in (LO_Y, HI_Y, LO_X, HI_X):

            @pl.when(sends[d])
            def _():
                if e > 0:
                    face_copy(e - 1, d).wait_send()
                face_copy(e, d).start()

    def take_faces(e):
        for d in range(4):
            pl.when(hears[d])(lambda: face_copy(e, d).wait_recv())

    def group_copy(k, slot, peer, src, slots):
        return pltpu.make_async_remote_copy(
            src_ref=src,
            dst_ref=slots.at[slot],
            send_sem=group_send.at[k],
            recv_sem=group_recv.at[k],
            device_id=peer,
            device_id_type=MESH,
        )

    def group_all(k, peer, slots, low, count):
        held = slots.at[pl.ds(low, count)]
        return pltpu.make_async_remote_copy(
            src_ref=held,
            dst_ref=held,
            send_sem=group_send.at[k],
            recv_sem=group_recv.at[k],
            device_id=peer(low),
            device_id_type=MESH,
        )

    def plane_start(k, src, slots):
        pl.loop(1, plane)(lambda p: group_copy(k, p, plane_peer(p), src, slots).start())

    def plane_all(k, slots):
        return group_all(k, plane_peer, slots, 1, plane - 1)

    def ring_start(k, src, slots):
        pl.loop(1, RING)(lambda p: group_copy(k, p, z_peer(p), src, slots).start())

    def ring_all(k, slots):
        return group_all(k, z_peer, slots, 1, RING - 1)

    pl.semaphore_wait(barrier, (window - 1) + (RING - 1) + (plane - 1))
    window_each(
        lambda q, slot: group_copy(0, slot, window_peer(q), own.at[0], slot_w).start()
    )
    send_faces(INPUT)

    lane_z = lax.broadcasted_iota(jnp.int32, (cols, layers), 1)
    col_y = lax.broadcasted_iota(jnp.int32, (cols, layers), 0)
    inner_z = lane_z < layers - 1
    inner_y = col_y < cols - 1

    def next_y(v):
        return pltpu.roll(v, cols - 1, 0)

    def last_y(v):
        return pltpu.roll(v, 1, 0)

    def next_z(v):
        return pltpu.roll(v, layers - 1, 1)

    def last_z(v):
        return pltpu.roll(v, 1, 1)

    def place(chosen, weights):
        return lax.dot_general(
            chosen,
            spots[...] * weights,
            (((1,), (1,)), ((), ())),
            precision=HIGHEST,
            preferred_element_type=jnp.float32,
        )

    loads[3].wait()
    largest = jnp.zeros((1, 128), jnp.float32)
    for b in range(cols // BLOCK):
        lower = fac[b]
        gram = lax.dot_general(
            lower,
            lower,
            (((0,), (0,)), ((), ())),
            precision=HIGHEST,
            preferred_element_type=jnp.float32,
        )
        high = gram.astype(jnp.bfloat16)
        prod_hi[b] = high
        prod_lo[b] = (gram - high.astype(jnp.float32)).astype(jnp.bfloat16)
        row_sum = jnp.sum(jnp.abs(gram), axis=0, keepdims=True)
        largest = jnp.maximum(largest, jnp.max(row_sum, axis=1, keepdims=True))
    own[1] = largest
    plane_start(1, own.at[1], slot_a.at[0])

    well_d[...] = place(select[pl.ds(0, cells), :], is_producer)
    well_e[...] = place(select[pl.ds(0, cells), :], pressure_row)

    zero_row = jnp.zeros((cols, layers), jnp.float32)

    def flux_row(x, flux_last):
        here, there = row(x), row(jnp.minimum(x + 1, rows - 1))
        k, p, f = perm[here, :], prs[here, :], frac[here, :]
        kx, px, fx = perm[there, :], prs[there, :], frac[there, :]
        tx = harmonic(k, kx)
        ty = jnp.where(inner_y, harmonic(k, next_y(k)), 0.0)
        tz = jnp.where(inner_z, 0.1 * harmonic(k, next_z(k)), 0.0)
        face_x[here, :] = tx
        face_y[here, :] = ty
        face_z[here, :] = tz
        wx = upwind(tx, p, px, f, fx)
        wy = upwind(ty, p, next_y(p), f, next_y(f))
        wz = upwind(tz, p, next_z(p), f, next_z(f))
        s = sat[here, :]
        made = 2.0 * s * s * (p * well_d[here, :] - well_e[here, :])
        moved[here, :] = s - dtp[here, :] * (
            made + (wx - flux_last) + (wy - last_y(wy)) + (wz - last_z(wz))
        )
        return wx

    lax.fori_loop(0, rows, flux_row, zero_row)

    def fraction(s):
        water, t = mobility(s)
        return water / t

    first, final = pl.ds(0, cols), pl.ds(cells - cols, cols)
    take_faces(INPUT)
    t = harmonic(input_x[0, PERM], perm[first, :])
    low_x[...] = t
    moved[first, :] += dtp[first, :] * upwind(
        t, input_x[0, PRS], prs[first, :], fraction(input_x[0, SAT]), frac[first, :]
    )
    t = harmonic(perm[final, :], input_x[1, PERM])
    face_x[final, :] = t
    moved[final, :] -= dtp[final, :] * upwind(
        t, prs[final, :], input_x[1, PRS], frac[final, :], fraction(input_x[1, SAT])
    )
    pack, rim = input_pack, input_y
    t = harmonic(rim[0, PERM], pack[0, PERM])
    side_y[0] = t
    flux = upwind(t, rim[0, PRS], pack[0, PRS], fraction(rim[0, SAT]), fraction(pack[0, SAT]))
    add_to(moved, 0, pack[0, DTP] * flux)
    t = harmonic(pack[1, PERM], rim[1, PERM])
    side_y[1] = t
    flux = upwind(t, pack[1, PRS], rim[1, PRS], fraction(pack[1, SAT]), fraction(rim[1, SAT]))
    add_to(moved, cols - 1, -pack[1, DTP] * flux)
    for i, c in ((0, 0), (1, cols - 1)):
        pack_y[MOVED - 1, i] = take(moved, c)
    send_faces(MOVED)

    plane_all(1, slot_a.at[0]).wait_recv()
    slot_a[0, 0] = own[1]
    own[2] = jnp.max(slot_a[0], axis=0)
    ring_start(2, own.at[2], slot_b.at[0])

    group_all(0, window_peer, slot_w, 0, window - 1).wait_recv()
    slot_w[window - 1] = own[0]
    sums = jnp.sum(slot_w[...], axis=0)
    scale = jnp.where(sums > 0.0, rate_row / jnp.where(sums > 0.0, sums, 1.0), 0.0)
    source[...] = place(select[...], scale)

    @pl.loop(0, rows)
    def _(x):
        here = row(x)
        made = mob[here, :] * source[here, :]
        s = moved[here, :] + dtp[here, :] * made
        satn[here, :] = s
        resid[here, :] = made
        total[here, :] = mobility(s)[1]

    store_satn = pltpu.make_async_copy(satn, made_hbm.at[0], store_sem.at[0])
    store_satn.start()

    def residual_row(x, flux_last):
        here, there = row(x), row(jnp.minimum(x + 1, rows - 1))
        t, tx = total[here, :], total[there, :]
        p, px = prs[here, :], prs[there, :]
        cx = face_x[here, :] * (0.5 * (t + tx))
        cy = face_y[here, :] * (0.5 * (t + next_y(t)))
        cz = face_z[here, :] * (0.5 * (t + next_z(t)))

        @pl.when(x < rows - 1)
        def _():
            face_x[here, :] = cx

        face_y[here, :] = cy
        face_z[here, :] = cz
        d, e = well_d[here, :], well_e[here, :]
        diag[here, :] = poro[here, :] + d * t
        fx = cx * (p - px)
        fy = cy * (p - next_y(p))
        fz = cz * (p - next_z(p))
        resid[here, :] = (
            resid[here, :]
            + t * (e - d * p)
            - ((fx - flux_last) + (fy - last_y(fy)) + (fz - last_z(fz)))
        )
        return fx

    lax.fori_loop(0, rows, residual_row, zero_row)

    def rim_total(before, sat_rim, dtp_rim, weights):
        s = before + dtp_rim * (mobility(sat_rim)[1] * weights)
        return mobility(s)[1]

    pack_total = [take(total, 0), take(total, cols - 1)]
    take_faces(MOVED)
    t = rim_total(
        halo_x[MOVED - 1, 0], input_x[0, SAT], input_x[0, DTP], source[pl.ds(cells, cols), :]
    )
    c = low_x[...] * (0.5 * (total[first, :] + t))
    low_x[...] = c
    resid[first, :] -= c * (prs[first, :] - input_x[0, PRS])
    t = rim_total(
        halo_x[MOVED - 1, 1],
        input_x[1, SAT],
        input_x[1, DTP],
        source[pl.ds(cells + cols, cols), :],
    )
    c = face_x[final, :] * (0.5 * (total[final, :] + t))
    face_x[final, :] = c
    resid[final, :] -= c * (prs[final, :] - input_x[1, PRS])
    for i, at in ((0, 0), (1, cols - 1)):
        t = rim_total(
            halo_y[MOVED - 1, i],
            rim[i, SAT],
            rim[i, DTP],
            source[pl.ds(rim_y + i * rows, rows), :],
        )
        c = side_y[i] * (0.5 * (pack_total[i] + t))
        side_y[i] = c
        add_to(resid, at, -c * (pack[i, PRS] - rim[i, PRS]))

    ring_all(2, slot_b.at[0]).wait_recv()
    slot_b[0, 0] = own[2]
    norm = 1.0 / jnp.max(slot_b[0], axis=0)
    norm = jnp.concatenate([norm] * (layers // 128), axis=1)

    def precondition(src, dst, factor):
        for b in range(cols // BLOCK):
            parts = [
                src[pl.ds(x * cols + b * BLOCK, BLOCK), :] for x in range(rows)
            ]
            v = jnp.concatenate(parts, axis=0) * factor
            high = v.astype(jnp.bfloat16)
            low = (v - high.astype(jnp.float32)).astype(jnp.bfloat16)
            z = jnp.dot(high, prod_hi[b], preferred_element_type=jnp.float32)
            z += jnp.dot(high, prod_lo[b], preferred_element_type=jnp.float32)
            z += jnp.dot(low, prod_hi[b], preferred_element_type=jnp.float32)
            for x in range(rows):
                dst[pl.ds(x * cols + b * BLOCK, BLOCK), :] = z[x * BLOCK : (x + 1) * BLOCK]

    stores = [store_satn]
    for k in range(BASIS):
        e = BASE + k
        vec, img = base.at[k], image.at[k]
        precondition(
            resid if k == 0 else image.at[k - 1], vec, norm if k == 0 else norm * SHIFT
        )
        pack_y[e - 1, 0] = take(vec, 0)
        pack_y[e - 1, 1] = take(vec, cols - 1)
        send_faces(e)
        store = pltpu.make_async_copy(vec, made_hbm.at[1 + k], store_sem.at[1 + k])
        store.start()
        stores.append(store)

        def image_row(x, flux_last, vec=vec, img=img):
            here, there = row(x), row(jnp.minimum(x + 1, rows - 1))
            v, vx = vec[here, :], vec[there, :]
            fx = face_x[here, :] * (v - vx)
            fy = face_y[here, :] * (v - next_y(v))
            fz = face_z[here, :] * (v - next_z(v))
            img[here, :] = (
                diag[here, :] * v
                + (fx - flux_last)
                + (fy - last_y(fy))
                + (fz - last_z(fz))
            )
            return fx

        lax.fori_loop(0, rows, image_row, zero_row)
        take_faces(e)
        h = e - 1
        img[first, :] += low_x[...] * (vec[first, :] - halo_x[h, 0])
        img[final, :] += face_x[final, :] * (vec[final, :] - halo_x[h, 1])
        for i, at in ((0, 0), (1, cols - 1)):
            add_to(img, at, side_y[i] * (pack_y[h, i] - halo_y[h, i]))

    pairs = [(0, 0), (1, 0), (1, 1), (2, 0), (2, 1), (2, 2)]

    def dots_row(x, sums):
        here = row(x)
        v = [base[k, here, :] for k in range(BASIS)]
        u = [image[k, here, :] for k in range(BASIS)]
        r = resid[here, :]
        terms = [v[i] * u[j] for i, j in pairs] + [v[i] * r for i in range(BASIS)]
        out = []
        for s, term in zip(sums, terms):
            for i in range(cols // 8):
                s = s + term[8 * i : 8 * i + 8]
            out.append(s)
        return tuple(out)

    zero_sum = jnp.zeros((8, layers), jnp.float32)
    count = len(pairs) + BASIS
    sums = lax.fori_loop(0, rows, dots_row, (zero_sum,) * count)
    message = jnp.zeros((1, 128), jnp.float32)
    for i, s in enumerate(sums):
        s = jnp.sum(s, axis=0, keepdims=True)
        message = jnp.where(lane == i, jnp.sum(s, axis=1, keepdims=True), message)
    own[3] = message
    plane_start(3, own.at[3], slot_a.at[1])
    plane_all(3, slot_a.at[1]).wait_recv()
    slot_a[1, 0] = own[3]
    own[4] = jnp.sum(slot_a[1], axis=0)
    ring_start(4, own.at[4], slot_b.at[1])
    ring_all(4, slot_b.at[1]).wait_recv()
    slot_b[1, 0] = own[4]
    result = jnp.sum(slot_b[1], axis=0)
    val = [result[:, i : i + 1] for i in range(count)]
    g00, g10, g11, g20, g21, g22, b0, b1, b2 = val

    def ratio(a, b):
        good = b > 0.0
        return jnp.where(good, a / jnp.where(good, b, 1.0), 0.0)

    l10, l20 = ratio(g10, g00), ratio(g20, g00)
    d1 = g11 - l10 * g10
    e21 = g21 - l20 * g10
    l21 = ratio(e21, d1)
    d2 = g22 - l20 * g20 - l21 * e21
    y1 = b1 - l10 * b0
    y2 = b2 - l20 * b0 - l21 * y1
    c2 = ratio(y2, d2)
    c1 = ratio(y1, d1) - l21 * c2
    c0 = ratio(b0, g00) - l10 * c1 - l20 * c2
    for k, c in enumerate((c0, c1, c2)):
        coef_out[k] = jnp.broadcast_to(c, (1, layers))

    group_all(0, window_peer, slot_w, 0, window - 1).wait_send()
    plane_all(1, slot_a.at[0]).wait_send()
    ring_all(2, slot_b.at[0]).wait_send()
    plane_all(3, slot_a.at[1]).wait_send()
    ring_all(4, slot_b.at[1]).wait_send()
    for d in range(4):
        pl.when(sends[d])(lambda: face_copy(EXCHANGES - 1, d).wait_send())
    for store in stores:
        store.wait()


def solution(mesh):
    n_gx, n_gy = mesh.shape["gx"], mesh.shape["gy"]

    def per_device(
        rock_type,
        perm_table,
        poro_table,
        saturation,
        pressure_old,
        factor_inverse,
        inject_cells,
        inject_index,
        inject_rate,
        produce_cells,
        produce_index,
        produce_pressure,
    ):
        rows, cols, layers = saturation.shape
        cells = rows * cols
        blocks = cols // BLOCK
        f32, bf16 = jnp.float32, jnp.bfloat16
        flat = (cells, layers)
        field = pltpu.VMEM(flat, f32)
        smem = pl.BlockSpec(memory_space=pltpu.SMEM)
        vmem = pl.BlockSpec(memory_space=pltpu.VMEM)
        hbm = pl.BlockSpec(memory_space=pl.ANY)
        plane = n_gx * (n_gy // RING)
        dma = pltpu.SemaphoreType.DMA
        window = (2 * REACH_X + 1) * (2 * REACH_Y + 1)
        scratch = [
            pltpu.VMEM((4,) + flat, f32),
            pltpu.VMEM(flat, jnp.int32),
            pltpu.VMEM((blocks, layers, layers), f32),
            pltpu.VMEM((blocks, layers, layers), bf16),
            pltpu.VMEM((blocks, layers, layers), bf16),
            field,
            field,
            field,
            pltpu.VMEM((cells + 2 * cols + 2 * rows, 128), f32),
            pltpu.VMEM((layers, 128), f32),
            field,
            field,
            field,
            pltpu.VMEM((cols, layers), f32),
            pltpu.VMEM((2, rows, layers), f32),
            field,
            field,
            field,
            pltpu.VMEM((cells + 2 * cols + 2 * rows, layers), f32),
            field,
            field,
            field,
            field,
            pltpu.VMEM((BASIS,) + flat, f32),
            pltpu.VMEM((BASIS,) + flat, f32),
            pltpu.VMEM((2, 4, cols, layers), f32),
            pltpu.VMEM((2, 4, rows, layers), f32),
            pltpu.VMEM((2, 4, rows, layers), f32),
            pltpu.VMEM((EXCHANGES - 1, 2, cols, layers), f32),
            pltpu.VMEM((EXCHANGES - 1, 2, rows, layers), f32),
            pltpu.VMEM((EXCHANGES - 1, 2, rows, layers), f32),
            pltpu.VMEM((5, 1, 128), f32),
            pltpu.VMEM((window, 1, 128), f32),
            pltpu.VMEM((2, plane, 1, 128), f32),
            pltpu.VMEM((2, RING, 1, 128), f32),
            dma((4,)),
            dma((1 + BASIS,)),
            dma((4,)),
            dma((2, 4)),
            dma((5,)),
            dma((5,)),
        ]
        made, coef = pl.pallas_call(
            functools.partial(kernel, (rows, cols, layers, n_gx, n_gy)),
            out_shape=[
                jax.ShapeDtypeStruct((1 + BASIS,) + flat, f32),
                jax.ShapeDtypeStruct((BASIS, 1, layers), f32),
            ],
            in_specs=[smem] * 6 + [vmem] * 2 + [hbm] * 4,
            out_specs=[hbm, vmem],
            scratch_shapes=scratch,
            compiler_params=pltpu.CompilerParams(
                collective_id=0, has_side_effects=True, vmem_limit_bytes=60 * 1024 * 1024
            ),
            name="reservoir_step",
        )(
            jnp.swapaxes(inject_cells, 1, 2),
            inject_rate,
            jnp.swapaxes(produce_cells, 1, 2),
            produce_pressure,
            perm_table,
            poro_table,
            inject_index,
            produce_index,
            rock_type.reshape(flat),
            saturation.reshape(flat),
            pressure_old.reshape(flat),
            factor_inverse.reshape(blocks, layers, layers),
        )
        change = coef[0] * made[1] + coef[1] * made[2] + coef[2] * made[3]
        pressure = pressure_old.reshape(flat) + change
        return made[0].reshape(saturation.shape), pressure.reshape(saturation.shape)

    grid = P("gx", "gy", None)
    in_specs = (grid, P(), P(), grid, grid, P("gx", "gy", None, None)) + (P(),) * 6
    return jax.shard_map(
        per_device, mesh=mesh, in_specs=in_specs, out_specs=(grid, grid), check_vma=False
    )
```

time: 55.2 us -> 52.6 us (0.953)
  Pallas kernels: 51.7 us -> 48.2 us
  other arithmetic: 0 us -> 0.97 us
    pallas_call x1, Pallas kernels: 51.7 us -> 48.2 us  [per_device(): pl.pallas_call(functools.partial(kernel, (rows, cols, layers, n_gx, n_gy)...]
    unnamed x4, local copies, waits for them, and re-layouts: 2.74 us -> 0.01 us
    slice x0 -> x2, local copies, waits for them, and re-layouts: none -> 2.5 us  [per_device(): change = coef[0] * made[1] + coef[1] * made[2] + coef[2] * made[3]]
    add x0 -> x1, other arithmetic: none -> 0.97 us  [per_device(): pressure = pressure_old.reshape(flat) + change]
where the time goes in v2:
time: 52.6 us; the launch traced here: 52.4 us
  Pallas kernels  48.2 us (92%)
  local copies, waits for them, and re-layouts  2.51 us (5%)
  other arithmetic  0.97 us (2%)
  between operations  0.66 us (1%)
    pallas_call x1, Pallas kernels, per_device(): pl.pallas_call(functools.partial(kernel, (rows, cols, layers, n_gx, n_gy)...  48.2 us
    slice x2, local copies, waits for them, and re-layouts, per_device(): change = coef[0] * made[1] + coef[1] * made[2] + coef[2] * made[3]  2.5 us

profile of v2, /device:TPU:1, one launch (start us, length us, event | category | flops | bytes accessed | tf_op | source)
XLA Modules:
  0.0 52.4 jit_solution(8641211537952818428)
XLA Ops:
  0.6 48.2 %reservoir_step.1 = (f32[4,512,256]{2,1,0:T(8,128)}, f32[3,1,256]{2,1,0:T(1,128)}) custom-call(s32[4,2,128]{2,1,0:T(2,128)} %bitcast.22, f32[4]{0:T(128)} %inj_rate.1, s32[8,2,128]{2,1,0:T(2,128)} %bitcast.21, f32[8]{0:T(128)} %pro_pressure.1, f32[8]{0:T(128)} %perm_table.1, f32[8]{0:T(128)} %poro_table.1, f32[4,128]{1,0:T(4,128)} %inj_index.1, ...), custom_call_target="tpu_custom_call" | custom-call | tf_op jit(solution)/shard_map/reservoir_step/pallas_call | solution.py:719
  48.9 0.0 copy-start.1
  48.9 0.0 copy-start
  48.9 2.5 %fusion = (f32[1,512,256]{2,1,0:T(8,128)S(1)}, f32[1,512,256]{2,1,0:T(8,128)S(1)}, f32[1,512,256]{2,1,0:T(8,128)S(1)}, f32[1,512,256]{2,1,0:T(8,128)}) fusion(f32[4,512,256]{2,1,0:T(8,128)} %get-tuple-element.4), kind=kLoop, calls=%fused_computation.1 | loop fusion | bytes 4194304 | tf_op jit(solution)/shard_map/slice | solution.py:746
  51.4 0.0 copy-done.1
  51.4 0.0 copy-done
  51.4 1.0 %add_add_fusion = f32[16,32,256]{2,1,0:T(8,128)} fusion(f32[16,32,256]{2,1,0:T(8,128)S(1)} %copy-done, f32[16,32,256]{2,1,0:T(8,128)S(1)} %bitcast.15, f32[16,32,256]{2,1,0:T(8,128)S(1)} %bitcast.16, f32[16,32,256]{2,1,0:T(8,128)S(1)} %bitcast.14, f32[256]{0:T(256)S(1)} %bitcast.24, f32[256]{0:T(256)S(1)} %bitcast.25, f32[256]{0:T(256)S(1)} %bitcast.23), kind=kLoop, calls=%fused_computation | loop fusion | flops 786432 | bytes 2624512 | tf_op jit(solution)/shard_map/add | solution.py:747
  (1 shorter events, 0.0 us)
Async XLA Ops:
  48.9 2.5 %copy-start.1 = (f32[3,1,256]{2,1,0:T(1,128)S(1)}, f32[3,1,256]{2,1,0:T(1,128)}, u32[]{:S(2)}) copy-start(f32[3,1,256]{2,1,0:T(1,128)} %get-tuple-element.5) | copy-start | bytes 9220
  48.9 2.5 %copy-start = (f32[16,32,256]{2,1,0:T(8,128)S(1)}, f32[16,32,256]{2,1,0:T(8,128)}, u32[]{:S(2)}) copy-start(f32[16,32,256]{2,1,0:T(8,128)} %param.16) | copy-start | bytes 1572868

commit v3 on v2

--- a/solution.py
+++ b/solution.py
@@ -45,7 +45,10 @@
     sat_hbm,
     prs_hbm,
     fac_hbm,
-    made_hbm,
+    satn_out,
+    z0_out,
+    z1_out,
+    z2_out,
     coef_out,
     inp,
     rock,
@@ -464,7 +467,7 @@
         resid[here, :] = made
         total[here, :] = mobility(s)[1]
 
-    store_satn = pltpu.make_async_copy(satn, made_hbm.at[0], store_sem.at[0])
+    store_satn = pltpu.make_async_copy(satn, satn_out, store_sem.at[0])
     store_satn.start()
 
     def residual_row(x, flux_last):
@@ -556,7 +559,9 @@
         pack_y[e - 1, 0] = take(vec, 0)
         pack_y[e - 1, 1] = take(vec, cols - 1)
         send_faces(e)
-        store = pltpu.make_async_copy(vec, made_hbm.at[1 + k], store_sem.at[1 + k])
+        store = pltpu.make_async_copy(
+            vec, (z0_out, z1_out, z2_out)[k], store_sem.at[1 + k]
+        )
         store.start()
         stores.append(store)
 
@@ -631,7 +636,7 @@
     c1 = ratio(y1, d1) - l21 * c2
     c0 = ratio(b0, g00) - l10 * c1 - l20 * c2
     for k, c in enumerate((c0, c1, c2)):
-        coef_out[k] = jnp.broadcast_to(c, (1, layers))
+        coef_out[k : k + 1, :] = jnp.broadcast_to(c, (1, layers))
 
     group_all(0, window_peer, slot_w, 0, window - 1).wait_send()
     plane_all(1, slot_a.at[0]).wait_send()
@@ -669,7 +674,8 @@
         field = pltpu.VMEM(flat, f32)
         smem = pl.BlockSpec(memory_space=pltpu.SMEM)
         vmem = pl.BlockSpec(memory_space=pltpu.VMEM)
-        hbm = pl.BlockSpec(memory_space=pl.ANY)
+        hbm = pl.BlockSpec(memory_space=pltpu.HBM)
+        out = pl.BlockSpec(memory_space=pl.ANY)
         plane = n_gx * (n_gy // RING)
         dma = pltpu.SemaphoreType.DMA
         window = (2 * REACH_X + 1) * (2 * REACH_Y + 1)
@@ -716,20 +722,7 @@
             dma((5,)),
             dma((5,)),
         ]
-        made, coef = pl.pallas_call(
-            functools.partial(kernel, (rows, cols, layers, n_gx, n_gy)),
-            out_shape=[
-                jax.ShapeDtypeStruct((1 + BASIS,) + flat, f32),
-                jax.ShapeDtypeStruct((BASIS, 1, layers), f32),
-            ],
-            in_specs=[smem] * 6 + [vmem] * 2 + [hbm] * 4,
-            out_specs=[hbm, vmem],
-            scratch_shapes=scratch,
-            compiler_params=pltpu.CompilerParams(
-                collective_id=0, has_side_effects=True, vmem_limit_bytes=60 * 1024 * 1024
-            ),
-            name="reservoir_step",
-        )(
+        operands = (
             jnp.swapaxes(inject_cells, 1, 2),
             inject_rate,
             jnp.swapaxes(produce_cells, 1, 2),
@@ -743,9 +736,23 @@
             pressure_old.reshape(flat),
             factor_inverse.reshape(blocks, layers, layers),
         )
-        change = coef[0] * made[1] + coef[1] * made[2] + coef[2] * made[3]
+        satn, z0, z1, z2, coef = pl.pallas_call(
+            functools.partial(kernel, (rows, cols, layers, n_gx, n_gy)),
+            out_shape=[
+                *[jax.ShapeDtypeStruct(flat, f32)] * (1 + BASIS),
+                jax.ShapeDtypeStruct((BASIS, layers), f32),
+            ],
+            in_specs=[smem] * 6 + [vmem] * 2 + [hbm] * 4,
+            out_specs=[out] * (1 + BASIS) + [vmem],
+            scratch_shapes=scratch,
+            compiler_params=pltpu.CompilerParams(
+                collective_id=0, has_side_effects=True, vmem_limit_bytes=24 * 1024 * 1024
+            ),
+            name="reservoir_step",
+        )(*(pltpu.with_memory_space_constraint(a, pltpu.HBM) for a in operands))
+        change = coef[0:1] * z0 + coef[1:2] * z1 + coef[2:3] * z2
         pressure = pressure_old.reshape(flat) + change
-        return made[0].reshape(saturation.shape), pressure.reshape(saturation.shape)
+        return satn.reshape(saturation.shape), pressure.reshape(saturation.shape)
 
     grid = P("gx", "gy", None)
     in_specs = (grid, P(), P(), grid, grid, P("gx", "gy", None, None)) + (P(),) * 6

time: 52.6 us -> 50.3 us (0.956)
  local copies, waits for them, and re-layouts: 2.51 us -> 0.8 us
    slice x2 -> x1, local copies, waits for them, and re-layouts: 2.5 us -> 0.01 us  [per_device(): change = coef[0:1] * z0 + coef[1:2] * z1 + coef[2:3] * z2]
    unnamed x4 -> x3, local copies, waits for them, and re-layouts: 0.01 us -> 0.8 us
where the time goes in v3:
time: 50.3 us; the launch traced here: 50.2 us
  Pallas kernels  47.8 us (95%)
  other arithmetic  0.94 us (2%)
  local copies, waits for them, and re-layouts  0.8 us (2%)
  between operations  0.67 us (1%)
    pallas_call x1, Pallas kernels, per_device(): pl.pallas_call(functools.partial(kernel, (rows, cols, layers, n_gx, n_gy)...  47.8 us

profile of v3, /device:TPU:1, one launch (start us, length us, event | category | flops | bytes accessed | tf_op | source)
XLA Modules:
  0.0 50.2 jit_solution(6542370376728739525)
XLA Ops:
  0.6 0.0 copy-start
  0.6 47.8 %reservoir_step.1 = (f32[512,256]{1,0:T(8,128)S(1)}, f32[512,256]{1,0:T(8,128)S(1)}, f32[512,256]{1,0:T(8,128)S(1)}, f32[512,256]{1,0:T(8,128)S(1)}, f32[3,256]{1,0:T(4,128)S(1)}) custom-call(s32[4,2,128]{2,1,0:T(2,128)} %bitcast.19, f32[4]{0:T(128)} %inj_rate.1, s32[8,2,128]{2,1,0:T(2,128)} %bitcast.18, f32[8]{0:T(128)} %pro_pressure.1, f32[8]{0:T(128)} %perm_table.1, ...), custom_call_target="tpu_custom_call" | custom-call | tf_op jit(solution)/shard_map/reservoir_step/pallas_call | solution.py:739
  48.5 0.0 copy-done
  48.5 0.9 %add_add_fusion = f32[512,256]{1,0:T(8,128)} fusion(f32[512,256]{1,0:T(8,128)S(1)} %get-tuple-element.11, f32[512,256]{1,0:T(8,128)S(1)} %get-tuple-element.10, f32[512,256]{1,0:T(8,128)S(1)} %get-tuple-element.9, f32[256]{0:T(256)S(1)} %bitcast.21, f32[256]{0:T(256)S(1)} %bitcast.22, f32[256]{0:T(256)S(1)} %bitcast.20, f32[16,32,256]{2,1,0:T(8,128)S(1)} %copy-done), kind=kLoop, calls=%fused_computation | loop fusion | flops 786432 | bytes 2624512 | tf_op jit(solution)/shard_map/add | solution.py:754
  49.5 0.8 %copy.15 = f32[16,32,256]{2,1,0:T(8,128)} copy(f32[16,32,256]{2,1,0:T(8,128)S(1)} %bitcast.12) | data formatting | bytes 1048576
  (1 shorter events, 0.0 us)
Async XLA Ops:
  0.6 47.9 %copy-start = (f32[16,32,256]{2,1,0:T(8,128)S(1)}, f32[16,32,256]{2,1,0:T(8,128)}, u32[]{:S(2)}) copy-start(f32[16,32,256]{2,1,0:T(8,128)} %param.16) | copy-start | bytes 1572868

commit v4 on v3

--- a/solution.py
+++ b/solution.py
@@ -19,7 +19,10 @@
 EXCHANGES = BASE + BASIS
 SAT, PRS, PERM, DTP = 0, 1, 2, 3
 LO_X, HI_X, LO_Y, HI_Y = 0, 1, 2, 3
-REACH_X, REACH_Y = 1, 5
+REACH = 5
+FAR_X = (4, 3, 5, 2, 6, 1, 7)
+FAR_Y = (2, 1, 3)
+FAR_Z = (4, 3, 5, 2, 6, 1, 7)
 
 
 def harmonic(former, latter):
@@ -80,9 +83,14 @@
     input_pack,
     halo_x,
     halo_y,
+    pack_x,
     pack_y,
     own,
     slot_w,
+    slot_v,
+    slot_x,
+    slot_y,
+    slot_s,
     slot_a,
     slot_b,
     load_sem,
@@ -93,6 +101,7 @@
     group_recv,
 ):
     rows, cols, layers, n_gx, n_gy = sizes
+    blocks = cols // BLOCK
     cells = rows * cols
     full_cols = cols * n_gy
     n_y = n_gy // RING
@@ -119,6 +128,10 @@
         for x in range(rows):
             ref[pl.ds(x * cols + c, 1), :] += value[x : x + 1]
 
+    def put(ref, c, value):
+        for x in range(rows):
+            ref[pl.ds(x * cols + c, 1), :] = value[x : x + 1]
+
     neighbours = (
         (lax.rem(gx + n_gx - 1, n_gx), gy),
         (lax.rem(gx + 1, n_gx), gy),
@@ -128,26 +141,21 @@
     sends = (gx > 0, gx < n_gx - 1, gy > 0, gy < n_gy - 1)
     hears = (gx < n_gx - 1, gx > 0, gy < n_gy - 1, gy > 0)
 
-    def z_peer(p):
-        return (gx, yy * RING + lax.rem(zz + p, RING))
-
-    def plane_peer(p):
-        spot = lax.rem(spot_a + p, plane)
-        return (spot // n_y, lax.rem(spot, n_y) * RING + zz)
-
-    width = 2 * REACH_Y + 1
-    window = (2 * REACH_X + 1) * width
-    centre = window // 2
-
-    def window_peer(q):
-        return (
-            lax.rem(gx + n_gx - REACH_X + q // width, n_gx),
-            lax.rem(gy + n_gy - REACH_Y + lax.rem(q, width), n_gy),
-        )
-
-    def window_each(action):
-        pl.loop(0, centre)(lambda q: action(q, q))
-        pl.loop(centre + 1, window)(lambda q: action(q, q - 1))
+    def near(a, b, c=0):
+        y = lax.rem(yy + b, n_y) if b else yy
+        z = lax.rem(zz + c, RING) if c else zz
+        return (lax.rem(gx + a, n_gx) if a else gx, y * RING + z)
+
+    def along_gy(b):
+        return (gx, lax.rem(gy + n_gy + b, n_gy))
+
+    reach = [b for d in range(REACH, 0, -1) for b in (d, -d)]
+    line_peers = [along_gy(b) for b in reach]
+    side_peers = [near(n_gx - 1, 0), near(1, 0)]
+    x_peers = [near(a, 0) for a in FAR_X]
+    y_peers = [near(0, b) for b in FAR_Y]
+    z_peers = [near(0, 0, c) for c in FAR_Z]
+    plane_peers = [near(a, b) for a in FAR_X + (0,) for b in FAR_Y + (0,) if a or b]
 
     loads = [
         pltpu.make_async_copy(src, dst, load_sem.at[i])
@@ -163,9 +171,8 @@
     def greet(peer):
         pl.semaphore_signal(barrier, inc=1, device_id=peer, device_id_type=MESH)
 
-    window_each(lambda q, slot: greet(window_peer(q)))
-    pl.loop(1, RING)(lambda p: greet(z_peer(p)))
-    pl.loop(1, plane)(lambda p: greet(plane_peer(p)))
+    for peer in plane_peers + line_peers + z_peers:
+        greet(peer)
 
     def clear_x(at):
         input_x[at] = jnp.zeros(input_x.shape[1:], jnp.float32)
@@ -181,6 +188,108 @@
     pl.when(gx == n_gx - 1)(lambda: clear_x(1))
     pl.when(gy == 0)(lambda: clear_y(0))
     pl.when(gy == n_gy - 1)(lambda: clear_y(1))
+
+    def lookup(kind, table):
+        bit0 = (kind & 1) == 1
+        bit1 = (kind & 2) == 2
+        pairs = [jnp.where(bit0, table[2 * i + 1], table[2 * i]) for i in range(4)]
+        high = jnp.where(bit1, pairs[3], pairs[2])
+        return jnp.where(kind >= 4, high, jnp.where(bit1, pairs[1], pairs[0]))
+
+    def fill_row(x):
+        kind = rock[row(x), :]
+        perm[row(x), :] = lookup(kind, perm_table)
+        porosity = lookup(kind, poro_table)
+        poro[row(x), :] = porosity
+        dtp[row(x), :] = TIME_STEP / porosity
+
+    loads[1].wait()
+    for i, c in ((0, 0), (1, cols - 1)):
+        kind = take(rock, c)
+        input_pack[i, PERM] = lookup(kind, perm_table)
+        input_pack[i, DTP] = TIME_STEP / lookup(kind, poro_table)
+    fill_row(0)
+    fill_row(rows - 1)
+    loads[0].wait()
+    loads[2].wait()
+    for i, c in ((0, 0), (1, cols - 1)):
+        input_pack[i, SAT] = take(sat, c)
+        input_pack[i, PRS] = take(prs, c)
+
+    def face_copy(e, d):
+        if e == INPUT:
+            if d < 2:
+                src = inp.at[:, pl.ds(0 if d == LO_X else cells - cols, cols), :]
+                dst = input_x.at[1 - d]
+            else:
+                src, dst = input_pack.at[d - 2], input_y.at[3 - d]
+        else:
+            if d < 2:
+                at = pl.ds(0 if d == LO_X else cells - cols, cols)
+                src = moved.at[at, :] if e == MOVED else pack_x.at[e - BASE, d]
+                dst = halo_x.at[e - 1, 1 - d]
+            else:
+                src, dst = pack_y.at[e - 1, d - 2], halo_y.at[e - 1, 3 - d]
+        return pltpu.make_async_remote_copy(
+            src_ref=src,
+            dst_ref=dst,
+            send_sem=face_send.at[d],
+            recv_sem=face_recv.at[e % 2, d],
+            device_id=neighbours[d],
+            device_id_type=MESH,
+        )
+
+    def send_faces(e):
+        for d in (LO_Y, HI_Y, LO_X, HI_X):
+
+            @pl.when(sends[d])
+            def _():
+                if e > 0:
+                    face_copy(e - 1, d).wait_send()
+                face_copy(e, d).start()
+
+    def take_faces(e):
+        for d in range(4):
+            pl.when(hears[d])(lambda: face_copy(e, d).wait_recv())
+
+    class Group:
+        def __init__(self, k, peers, slots):
+            self.k, self.peers, self.slots = k, peers, slots
+
+        def copy(self, src, dst, peer):
+            return pltpu.make_async_remote_copy(
+                src_ref=src,
+                dst_ref=dst,
+                send_sem=group_send.at[self.k],
+                recv_sem=group_recv.at[self.k],
+                device_id=peer,
+                device_id_type=MESH,
+            )
+
+        def start(self, src):
+            for i, peer in enumerate(self.peers):
+                self.copy(src, self.slots.at[i], peer).start()
+
+        def whole(self):
+            held = self.slots.at[pl.ds(0, len(self.peers))]
+            return self.copy(held, held, self.peers[0])
+
+        def take(self, mine):
+            self.whole().wait_recv()
+            self.slots[len(self.peers)] = mine
+            return self.slots[...]
+
+    line = Group(0, line_peers, slot_w)
+    sides = Group(1, side_peers, slot_v)
+    scale_x = Group(2, x_peers, slot_x)
+    scale_y = Group(3, y_peers, slot_y)
+    scale_z = Group(4, z_peers, slot_s)
+    sum_plane = Group(5, plane_peers, slot_a)
+    sum_z = Group(6, z_peers, slot_b)
+    groups = (line, sides, scale_x, scale_y, scale_z, sum_plane, sum_z)
+
+    pl.semaphore_wait(barrier, len(plane_peers) + len(line_peers) + len(z_peers))
+    send_faces(INPUT)
 
     lane = lax.broadcasted_iota(jnp.int32, (1, 128), 1)
     well_row = jnp.full((1, 128), -9, jnp.int32)
@@ -228,7 +337,7 @@
         row_pos == well_row, column[8 + cols : 9 + cols], 0.0
     )
 
-    loads[0].wait()
+    pl.loop(1, rows - 1)(fill_row)
 
     def mobility(s):
         water = 2.0 * s * s
@@ -245,106 +354,7 @@
         mob[...], spots[...], precision=HIGHEST, preferred_element_type=jnp.float32
     )
     own[0] = jnp.sum(picked * select[pl.ds(0, cells), :], axis=0, keepdims=True)
-
-    loads[1].wait()
-
-    @pl.loop(0, rows)
-    def _(x):
-        kind = rock[row(x), :]
-        bit0 = (kind & 1) == 1
-        bit1 = (kind & 2) == 2
-        bit2 = kind >= 4
-
-        def lookup(table):
-            pairs = [jnp.where(bit0, table[2 * i + 1], table[2 * i]) for i in range(4)]
-            return jnp.where(
-                bit2, jnp.where(bit1, pairs[3], pairs[2]), jnp.where(bit1, pairs[1], pairs[0])
-            )
-
-        perm[row(x), :] = lookup(perm_table)
-        porosity = lookup(poro_table)
-        poro[row(x), :] = porosity
-        dtp[row(x), :] = TIME_STEP / porosity
-
-    loads[2].wait()
-    for i in range(4):
-        input_pack[0, i] = take(inp.at[i], 0)
-        input_pack[1, i] = take(inp.at[i], cols - 1)
-
-    def face_copy(e, d):
-        if e == INPUT:
-            if d < 2:
-                src = inp.at[:, pl.ds(0 if d == LO_X else cells - cols, cols), :]
-                dst = input_x.at[1 - d]
-            else:
-                src, dst = input_pack.at[d - 2], input_y.at[3 - d]
-        else:
-            field = moved if e == MOVED else base.at[e - BASE]
-            if d < 2:
-                src = field.at[pl.ds(0 if d == LO_X else cells - cols, cols), :]
-                dst = halo_x.at[e - 1, 1 - d]
-            else:
-                src, dst = pack_y.at[e - 1, d - 2], halo_y.at[e - 1, 3 - d]
-        return pltpu.make_async_remote_copy(
-            src_ref=src,
-            dst_ref=dst,
-            send_sem=face_send.at[d],
-            recv_sem=face_recv.at[e % 2, d],
-            device_id=neighbours[d],
-            device_id_type=MESH,
-        )
-
-    def send_faces(e):
-        for d in (LO_Y, HI_Y, LO_X, HI_X):
-
-            @pl.when(sends[d])
-            def _():
-                if e > 0:
-                    face_copy(e - 1, d).wait_send()
-                face_copy(e, d).start()
-
-    def take_faces(e):
-        for d in range(4):
-            pl.when(hears[d])(lambda: face_copy(e, d).wait_recv())
-
-    def group_copy(k, slot, peer, src, slots):
-        return pltpu.make_async_remote_copy(
-            src_ref=src,
-            dst_ref=slots.at[slot],
-            send_sem=group_send.at[k],
-            recv_sem=group_recv.at[k],
-            device_id=peer,
-            device_id_type=MESH,
-        )
-
-    def group_all(k, peer, slots, low, count):
-        held = slots.at[pl.ds(low, count)]
-        return pltpu.make_async_remote_copy(
-            src_ref=held,
-            dst_ref=held,
-            send_sem=group_send.at[k],
-            recv_sem=group_recv.at[k],
-            device_id=peer(low),
-            device_id_type=MESH,
-        )
-
-    def plane_start(k, src, slots):
-        pl.loop(1, plane)(lambda p: group_copy(k, p, plane_peer(p), src, slots).start())
-
-    def plane_all(k, slots):
-        return group_all(k, plane_peer, slots, 1, plane - 1)
-
-    def ring_start(k, src, slots):
-        pl.loop(1, RING)(lambda p: group_copy(k, p, z_peer(p), src, slots).start())
-
-    def ring_all(k, slots):
-        return group_all(k, z_peer, slots, 1, RING - 1)
-
-    pl.semaphore_wait(barrier, (window - 1) + (RING - 1) + (plane - 1))
-    window_each(
-        lambda q, slot: group_copy(0, slot, window_peer(q), own.at[0], slot_w).start()
-    )
-    send_faces(INPUT)
+    line.start(own.at[0])
 
     lane_z = lax.broadcasted_iota(jnp.int32, (cols, layers), 1)
     col_y = lax.broadcasted_iota(jnp.int32, (cols, layers), 0)
@@ -374,7 +384,7 @@
 
     loads[3].wait()
     largest = jnp.zeros((1, 128), jnp.float32)
-    for b in range(cols // BLOCK):
+    for b in range(blocks):
         lower = fac[b]
         gram = lax.dot_general(
             lower,
@@ -389,7 +399,7 @@
         row_sum = jnp.sum(jnp.abs(gram), axis=0, keepdims=True)
         largest = jnp.maximum(largest, jnp.max(row_sum, axis=1, keepdims=True))
     own[1] = largest
-    plane_start(1, own.at[1], slot_a.at[0])
+    scale_x.start(own.at[1])
 
     well_d[...] = place(select[pl.ds(0, cells), :], is_producer)
     well_e[...] = place(select[pl.ds(0, cells), :], pressure_row)
@@ -446,15 +456,12 @@
     for i, c in ((0, 0), (1, cols - 1)):
         pack_y[MOVED - 1, i] = take(moved, c)
     send_faces(MOVED)
-
-    plane_all(1, slot_a.at[0]).wait_recv()
-    slot_a[0, 0] = own[1]
-    own[2] = jnp.max(slot_a[0], axis=0)
-    ring_start(2, own.at[2], slot_b.at[0])
-
-    group_all(0, window_peer, slot_w, 0, window - 1).wait_recv()
-    slot_w[window - 1] = own[0]
-    sums = jnp.sum(slot_w[...], axis=0)
+    own[3] = jnp.sum(line.take(own[0]), axis=0)
+    sides.start(own.at[3])
+
+    own[2] = jnp.max(scale_x.take(own[1]), axis=0)
+    scale_y.start(own.at[2])
+    sums = jnp.sum(sides.take(own[3]), axis=0)
     scale = jnp.where(sums > 0.0, rate_row / jnp.where(sums > 0.0, sums, 1.0), 0.0)
     source[...] = place(select[...], scale)
 
@@ -503,6 +510,7 @@
         return mobility(s)[1]
 
     pack_total = [take(total, 0), take(total, cols - 1)]
+    edge = []
     take_faces(MOVED)
     t = rim_total(
         halo_x[MOVED - 1, 0], input_x[0, SAT], input_x[0, DTP], source[pl.ds(cells, cols), :]
@@ -528,37 +536,58 @@
         )
         c = side_y[i] * (0.5 * (pack_total[i] + t))
         side_y[i] = c
-        add_to(resid, at, -c * (pack[i, PRS] - rim[i, PRS]))
-
-    ring_all(2, slot_b.at[0]).wait_recv()
-    slot_b[0, 0] = own[2]
-    norm = 1.0 / jnp.max(slot_b[0], axis=0)
-    norm = jnp.concatenate([norm] * (layers // 128), axis=1)
+        edge.append(take(resid, at) - c * (pack[i, PRS] - rim[i, PRS]))
+        put(resid, at, edge[i])
+
+    def apply(v, b, factor):
+        if factor is not None:
+            v = v * factor
+        high = v.astype(jnp.bfloat16)
+        low = (v - high.astype(jnp.float32)).astype(jnp.bfloat16)
+        z = jnp.dot(high, prod_hi[b], preferred_element_type=jnp.float32)
+        z += jnp.dot(high, prod_lo[b], preferred_element_type=jnp.float32)
+        return z + jnp.dot(low, prod_hi[b], preferred_element_type=jnp.float32)
 
     def precondition(src, dst, factor):
-        for b in range(cols // BLOCK):
+        for b in range(blocks):
             parts = [
                 src[pl.ds(x * cols + b * BLOCK, BLOCK), :] for x in range(rows)
             ]
-            v = jnp.concatenate(parts, axis=0) * factor
-            high = v.astype(jnp.bfloat16)
-            low = (v - high.astype(jnp.float32)).astype(jnp.bfloat16)
-            z = jnp.dot(high, prod_hi[b], preferred_element_type=jnp.float32)
-            z += jnp.dot(high, prod_lo[b], preferred_element_type=jnp.float32)
-            z += jnp.dot(low, prod_hi[b], preferred_element_type=jnp.float32)
+            z = apply(jnp.concatenate(parts, axis=0), b, factor)
             for x in range(rows):
                 dst[pl.ds(x * cols + b * BLOCK, BLOCK), :] = z[x * BLOCK : (x + 1) * BLOCK]
+
+    def precondition_rim(k, src, low_column, high_column, factor):
+        for b in range(blocks):
+            here = pl.ds(b * BLOCK, BLOCK)
+            parts = [src[here, :], src[pl.ds(cells - cols + b * BLOCK, BLOCK), :]]
+            if b == 0:
+                parts.append(low_column)
+            if b == blocks - 1:
+                parts.append(high_column)
+            z = apply(jnp.concatenate(parts, axis=0), b, factor)
+            pack_x[k, 0, here, :] = z[:BLOCK]
+            pack_x[k, 1, here, :] = z[BLOCK : 2 * BLOCK]
+            if b == 0:
+                pack_y[BASE - 1 + k, 0] = z[2 * BLOCK : 2 * BLOCK + rows]
+            if b == blocks - 1:
+                pack_y[BASE - 1 + k, 1] = z[-rows:]
 
     stores = [store_satn]
     for k in range(BASIS):
         e = BASE + k
         vec, img = base.at[k], image.at[k]
-        precondition(
-            resid if k == 0 else image.at[k - 1], vec, norm if k == 0 else norm * SHIFT
-        )
-        pack_y[e - 1, 0] = take(vec, 0)
-        pack_y[e - 1, 1] = take(vec, cols - 1)
+        if k == 1:
+            top = jnp.max(scale_z.take(own[4]), axis=0)
+            norm = jnp.concatenate([1.0 / top] * (layers // 128), axis=1)
+        factor = (lambda: None, lambda: (SHIFT * norm) * norm, lambda: SHIFT * norm)[k]()
+        prior = resid if k == 0 else image.at[k - 1]
+        precondition_rim(k, prior, edge[0], edge[1], factor)
         send_faces(e)
+        if k == 0:
+            own[4] = jnp.max(scale_y.take(own[2]), axis=0)
+            scale_z.start(own.at[4])
+        precondition(prior, vec, factor)
         store = pltpu.make_async_copy(
             vec, (z0_out, z1_out, z2_out)[k], store_sem.at[1 + k]
         )
@@ -585,7 +614,8 @@
         img[first, :] += low_x[...] * (vec[first, :] - halo_x[h, 0])
         img[final, :] += face_x[final, :] * (vec[final, :] - halo_x[h, 1])
         for i, at in ((0, 0), (1, cols - 1)):
-            add_to(img, at, side_y[i] * (pack_y[h, i] - halo_y[h, i]))
+            edge[i] = take(img, at) + side_y[i] * (pack_y[h, i] - halo_y[h, i])
+            put(img, at, edge[i])
 
     pairs = [(0, 0), (1, 0), (1, 1), (2, 0), (2, 1), (2, 2)]
 
@@ -609,15 +639,11 @@
     for i, s in enumerate(sums):
         s = jnp.sum(s, axis=0, keepdims=True)
         message = jnp.where(lane == i, jnp.sum(s, axis=1, keepdims=True), message)
-    own[3] = message
-    plane_start(3, own.at[3], slot_a.at[1])
-    plane_all(3, slot_a.at[1]).wait_recv()
-    slot_a[1, 0] = own[3]
-    own[4] = jnp.sum(slot_a[1], axis=0)
-    ring_start(4, own.at[4], slot_b.at[1])
-    ring_all(4, slot_b.at[1]).wait_recv()
-    slot_b[1, 0] = own[4]
-    result = jnp.sum(slot_b[1], axis=0)
+    own[5] = message
+    sum_plane.start(own.at[5])
+    own[6] = jnp.sum(sum_plane.take(own[5]), axis=0)
+    sum_z.start(own.at[6])
+    result = jnp.sum(sum_z.take(own[6]), axis=0)
     val = [result[:, i : i + 1] for i in range(count)]
     g00, g10, g11, g20, g21, g22, b0, b1, b2 = val
 
@@ -638,11 +664,8 @@
     for k, c in enumerate((c0, c1, c2)):
         coef_out[k : k + 1, :] = jnp.broadcast_to(c, (1, layers))
 
-    group_all(0, window_peer, slot_w, 0, window - 1).wait_send()
-    plane_all(1, slot_a.at[0]).wait_send()
-    ring_all(2, slot_b.at[0]).wait_send()
-    plane_all(3, slot_a.at[1]).wait_send()
-    ring_all(4, slot_b.at[1]).wait_send()
+    for group in groups:
+        group.whole().wait_send()
     for d in range(4):
         pl.when(sends[d])(lambda: face_copy(EXCHANGES - 1, d).wait_send())
     for store in stores:
@@ -678,7 +701,6 @@
         out = pl.BlockSpec(memory_space=pl.ANY)
         plane = n_gx * (n_gy // RING)
         dma = pltpu.SemaphoreType.DMA
-        window = (2 * REACH_X + 1) * (2 * REACH_Y + 1)
         scratch = [
             pltpu.VMEM((4,) + flat, f32),
             pltpu.VMEM(flat, jnp.int32),
@@ -710,17 +732,22 @@
             pltpu.VMEM((2, 4, rows, layers), f32),
             pltpu.VMEM((EXCHANGES - 1, 2, cols, layers), f32),
             pltpu.VMEM((EXCHANGES - 1, 2, rows, layers), f32),
+            pltpu.VMEM((BASIS, 2, cols, layers), f32),
             pltpu.VMEM((EXCHANGES - 1, 2, rows, layers), f32),
-            pltpu.VMEM((5, 1, 128), f32),
-            pltpu.VMEM((window, 1, 128), f32),
-            pltpu.VMEM((2, plane, 1, 128), f32),
-            pltpu.VMEM((2, RING, 1, 128), f32),
+            pltpu.VMEM((7, 1, 128), f32),
+            pltpu.VMEM((2 * REACH + 1, 1, 128), f32),
+            pltpu.VMEM((3, 1, 128), f32),
+            pltpu.VMEM((n_gx, 1, 128), f32),
+            pltpu.VMEM((n_gy // RING, 1, 128), f32),
+            pltpu.VMEM((RING, 1, 128), f32),
+            pltpu.VMEM((plane, 1, 128), f32),
+            pltpu.VMEM((RING, 1, 128), f32),
             dma((4,)),
             dma((1 + BASIS,)),
             dma((4,)),
             dma((2, 4)),
-            dma((5,)),
-            dma((5,)),
+            dma((7,)),
+            dma((7,)),
         ]
         operands = (
             jnp.swapaxes(inject_cells, 1, 2),

time: 50.3 us -> 51.2 us (1.018)
  Pallas kernels: 47.8 us -> 48.7 us
    pallas_call x1, Pallas kernels: 47.8 us -> 48.7 us  [per_device(): pl.pallas_call(functools.partial(kernel, (rows, cols, layers, n_gx, n_gy)...]
where the time goes in v4:
time: 51.2 us; the launch traced here: 51.1 us
  Pallas kernels  48.7 us (95%)
  other arithmetic  0.94 us (2%)
  local copies, waits for them, and re-layouts  0.8 us (2%)
  between operations  0.67 us (1%)
    pallas_call x1, Pallas kernels, per_device(): pl.pallas_call(functools.partial(kernel, (rows, cols, layers, n_gx, n_gy)...  48.7 us

profile of v4, /device:TPU:1, one launch (start us, length us, event | category | flops | bytes accessed | tf_op | source)
XLA Modules:
  0.0 51.1 jit_solution(17595198327553295860)
XLA Ops:
  0.6 0.0 copy-start
  0.6 48.7 %reservoir_step.1 = (f32[512,256]{1,0:T(8,128)S(1)}, f32[512,256]{1,0:T(8,128)S(1)}, f32[512,256]{1,0:T(8,128)S(1)}, f32[512,256]{1,0:T(8,128)S(1)}, f32[3,256]{1,0:T(4,128)S(1)}) custom-call(s32[4,2,128]{2,1,0:T(2,128)} %bitcast.19, f32[4]{0:T(128)} %inj_rate.1, s32[8,2,128]{2,1,0:T(2,128)} %bitcast.18, f32[8]{0:T(128)} %pro_pressure.1, f32[8]{0:T(128)} %perm_table.1, ...), custom_call_target="tpu_custom_call" | custom-call | tf_op jit(solution)/shard_map/reservoir_step/pallas_call | solution.py:766
  49.3 0.0 copy-done
  49.3 0.9 %add_add_fusion = f32[512,256]{1,0:T(8,128)} fusion(f32[512,256]{1,0:T(8,128)S(1)} %get-tuple-element.11, f32[512,256]{1,0:T(8,128)S(1)} %get-tuple-element.10, f32[512,256]{1,0:T(8,128)S(1)} %get-tuple-element.9, f32[256]{0:T(256)S(1)} %bitcast.21, f32[256]{0:T(256)S(1)} %bitcast.22, f32[256]{0:T(256)S(1)} %bitcast.20, f32[16,32,256]{2,1,0:T(8,128)S(1)} %copy-done), kind=kLoop, calls=%fused_computation | loop fusion | flops 786432 | bytes 2624512 | tf_op jit(solution)/shard_map/add | solution.py:781
  50.3 0.8 %copy.15 = f32[16,32,256]{2,1,0:T(8,128)} copy(f32[16,32,256]{2,1,0:T(8,128)S(1)} %bitcast.12) | data formatting | bytes 1048576
  (1 shorter events, 0.0 us)
Async XLA Ops:
  0.6 48.7 %copy-start = (f32[16,32,256]{2,1,0:T(8,128)S(1)}, f32[16,32,256]{2,1,0:T(8,128)}, u32[]{:S(2)}) copy-start(f32[16,32,256]{2,1,0:T(8,128)} %param.16) | copy-start | bytes 1572868

commit v5 on v4

--- a/solution.py
+++ b/solution.py
@@ -8,9 +8,9 @@
 from jax.sharding import PartitionSpec as P
 
 MESH = pl.DeviceIdType.MESH
-HIGHEST = lax.Precision.HIGHEST
 BLOCK = 16
 BASIS = 3
+UNROLL = 4
 RING = 8
 TIME_STEP = 0.002
 SHIFT = 2.0**-14
@@ -67,6 +67,7 @@
     face_y,
     face_z,
     low_x,
+    high_x,
     side_y,
     moved,
     well_d,
@@ -87,7 +88,6 @@
     pack_y,
     own,
     slot_w,
-    slot_v,
     slot_x,
     slot_y,
     slot_s,
@@ -146,16 +146,33 @@
         z = lax.rem(zz + c, RING) if c else zz
         return (lax.rem(gx + a, n_gx) if a else gx, y * RING + z)
 
-    def along_gy(b):
-        return (gx, lax.rem(gy + n_gy + b, n_gy))
-
-    reach = [b for d in range(REACH, 0, -1) for b in (d, -d)]
-    line_peers = [along_gy(b) for b in reach]
-    side_peers = [near(n_gx - 1, 0), near(1, 0)]
+    def line(a, b):
+        return (lax.rem(gx + n_gx + a, n_gx), lax.rem(gy + n_gy + b, n_gy))
+
+    reach = [b for d in range(REACH, 0, -1) for b in (d, -d)] + [0]
+    window_peers = [line(a, b) for b in reach for a in (-1, 1, 0) if a or b]
     x_peers = [near(a, 0) for a in FAR_X]
     y_peers = [near(0, b) for b in FAR_Y]
     z_peers = [near(0, 0, c) for c in FAR_Z]
     plane_peers = [near(a, b) for a in FAR_X + (0,) for b in FAR_Y + (0,) if a or b]
+
+    def each_row(body, carry=None):
+        def step(i, kept):
+            for j in range(UNROLL):
+                kept = body(i * UNROLL + j, kept)
+            return kept
+
+        if carry is None:
+            pl.loop(0, rows // UNROLL)(lambda i: step(i, None) and None)
+        else:
+            lax.fori_loop(0, rows // UNROLL, step, carry)
+
+    def split(v):
+        high = v.astype(jnp.bfloat16)
+        return high, (v - high.astype(jnp.float32)).astype(jnp.bfloat16)
+
+    def product(a, b, dims):
+        return lax.dot_general(a, b, (dims, ((), ())), preferred_element_type=jnp.float32)
 
     loads = [
         pltpu.make_async_copy(src, dst, load_sem.at[i])
@@ -171,7 +188,7 @@
     def greet(peer):
         pl.semaphore_signal(barrier, inc=1, device_id=peer, device_id_type=MESH)
 
-    for peer in plane_peers + line_peers + z_peers:
+    for peer in plane_peers + window_peers + z_peers:
         greet(peer)
 
     def clear_x(at):
@@ -196,7 +213,7 @@
         high = jnp.where(bit1, pairs[3], pairs[2])
         return jnp.where(kind >= 4, high, jnp.where(bit1, pairs[1], pairs[0]))
 
-    def fill_row(x):
+    def fill_row(x, _=None):
         kind = rock[row(x), :]
         perm[row(x), :] = lookup(kind, perm_table)
         porosity = lookup(kind, poro_table)
@@ -279,16 +296,15 @@
             self.slots[len(self.peers)] = mine
             return self.slots[...]
 
-    line = Group(0, line_peers, slot_w)
-    sides = Group(1, side_peers, slot_v)
-    scale_x = Group(2, x_peers, slot_x)
-    scale_y = Group(3, y_peers, slot_y)
-    scale_z = Group(4, z_peers, slot_s)
-    sum_plane = Group(5, plane_peers, slot_a)
-    sum_z = Group(6, z_peers, slot_b)
-    groups = (line, sides, scale_x, scale_y, scale_z, sum_plane, sum_z)
-
-    pl.semaphore_wait(barrier, len(plane_peers) + len(line_peers) + len(z_peers))
+    window = Group(0, window_peers, slot_w)
+    scale_x = Group(1, x_peers, slot_x)
+    scale_y = Group(2, y_peers, slot_y)
+    scale_z = Group(3, z_peers, slot_s)
+    sum_plane = Group(4, plane_peers, slot_a)
+    sum_z = Group(5, z_peers, slot_b)
+    groups = (window, scale_x, scale_y, scale_z, sum_plane, sum_z)
+
+    pl.semaphore_wait(barrier, len(plane_peers) + len(window_peers) + len(z_peers))
     send_faces(INPUT)
 
     lane = lax.broadcasted_iota(jnp.int32, (1, 128), 1)
@@ -324,7 +340,7 @@
             rate_row = jnp.where(lane == w, inj_rate[i], rate_row)
     is_producer = jnp.where(lane < producers, 1.0, 0.0)
     layer_pos = lax.broadcasted_iota(jnp.int32, (layers, 128), 0)
-    spots[...] = jnp.where(layer_pos == well_layer, 1.0, 0.0)
+    spots[...] = jnp.where(layer_pos == well_layer, 1.0, 0.0).astype(jnp.bfloat16)
     own_column = column[8 : 8 + cols]
     for x in range(rows):
         select[x * cols : (x + 1) * cols, :] = jnp.where(well_row == x, own_column, 0.0)
@@ -337,24 +353,22 @@
         row_pos == well_row, column[8 + cols : 9 + cols], 0.0
     )
 
-    pl.loop(1, rows - 1)(fill_row)
 
     def mobility(s):
         water = 2.0 * s * s
         rest = 1.0 - s
         return water, water + rest * rest
 
-    @pl.loop(0, rows)
-    def _(x):
+    def mobility_row(x, _):
         water, t = mobility(sat[row(x), :])
         mob[row(x), :] = t
         frac[row(x), :] = water / t
 
-    picked = jnp.dot(
-        mob[...], spots[...], precision=HIGHEST, preferred_element_type=jnp.float32
-    )
+    each_row(mobility_row)
+    spot = spots[...]
+    picked = sum(product(v, spot, ((1,), (0,))) for v in split(mob[...]))
     own[0] = jnp.sum(picked * select[pl.ds(0, cells), :], axis=0, keepdims=True)
-    line.start(own.at[0])
+    window.start(own.at[0])
 
     lane_z = lax.broadcasted_iota(jnp.int32, (cols, layers), 1)
     col_y = lax.broadcasted_iota(jnp.int32, (cols, layers), 0)
@@ -373,36 +387,27 @@
     def last_z(v):
         return pltpu.roll(v, 1, 1)
 
-    def place(chosen, weights):
-        return lax.dot_general(
-            chosen,
-            spots[...] * weights,
-            (((1,), (1,)), ((), ())),
-            precision=HIGHEST,
-            preferred_element_type=jnp.float32,
-        )
+    def place(chosen):
+        return sum(product(v, spot, ((1,), (1,))) for v in split(chosen))
 
     loads[3].wait()
     largest = jnp.zeros((1, 128), jnp.float32)
     for b in range(blocks):
         lower = fac[b]
-        gram = lax.dot_general(
-            lower,
-            lower,
-            (((0,), (0,)), ((), ())),
-            precision=HIGHEST,
-            preferred_element_type=jnp.float32,
-        )
-        high = gram.astype(jnp.bfloat16)
-        prod_hi[b] = high
-        prod_lo[b] = (gram - high.astype(jnp.float32)).astype(jnp.bfloat16)
+        high, low = split(lower)
+        over = ((0,), (0,))
+        gram = product(high, high, over) + product(high, low, over) + product(low, high, over)
+        prod_hi[b], prod_lo[b] = split(gram)
         row_sum = jnp.sum(jnp.abs(gram), axis=0, keepdims=True)
         largest = jnp.maximum(largest, jnp.max(row_sum, axis=1, keepdims=True))
     own[1] = largest
     scale_x.start(own.at[1])
 
-    well_d[...] = place(select[pl.ds(0, cells), :], is_producer)
-    well_e[...] = place(select[pl.ds(0, cells), :], pressure_row)
+    for x in range(1, rows - 1):
+        fill_row(x)
+    chosen = select[pl.ds(0, cells), :]
+    well_d[...] = place(chosen * is_producer)
+    well_e[...] = place(chosen * pressure_row)
 
     zero_row = jnp.zeros((cols, layers), jnp.float32)
 
@@ -426,7 +431,7 @@
         )
         return wx
 
-    lax.fori_loop(0, rows, flux_row, zero_row)
+    each_row(flux_row, zero_row)
 
     def fraction(s):
         water, t = mobility(s)
@@ -440,7 +445,7 @@
         t, input_x[0, PRS], prs[first, :], fraction(input_x[0, SAT]), frac[first, :]
     )
     t = harmonic(perm[final, :], input_x[1, PERM])
-    face_x[final, :] = t
+    high_x[...] = t
     moved[final, :] -= dtp[final, :] * upwind(
         t, prs[final, :], input_x[1, PRS], frac[final, :], fraction(input_x[1, SAT])
     )
@@ -456,23 +461,22 @@
     for i, c in ((0, 0), (1, cols - 1)):
         pack_y[MOVED - 1, i] = take(moved, c)
     send_faces(MOVED)
-    own[3] = jnp.sum(line.take(own[0]), axis=0)
-    sides.start(own.at[3])
 
     own[2] = jnp.max(scale_x.take(own[1]), axis=0)
     scale_y.start(own.at[2])
-    sums = jnp.sum(sides.take(own[3]), axis=0)
+    sums = jnp.sum(window.take(own[0]), axis=0)
     scale = jnp.where(sums > 0.0, rate_row / jnp.where(sums > 0.0, sums, 1.0), 0.0)
-    source[...] = place(select[...], scale)
-
-    @pl.loop(0, rows)
-    def _(x):
+    source[...] = place(select[...] * scale)
+
+    def moved_row(x, _):
         here = row(x)
         made = mob[here, :] * source[here, :]
         s = moved[here, :] + dtp[here, :] * made
         satn[here, :] = s
         resid[here, :] = made
         total[here, :] = mobility(s)[1]
+
+    each_row(moved_row)
 
     store_satn = pltpu.make_async_copy(satn, satn_out, store_sem.at[0])
     store_satn.start()
@@ -484,11 +488,7 @@
         cx = face_x[here, :] * (0.5 * (t + tx))
         cy = face_y[here, :] * (0.5 * (t + next_y(t)))
         cz = face_z[here, :] * (0.5 * (t + next_z(t)))
-
-        @pl.when(x < rows - 1)
-        def _():
-            face_x[here, :] = cx
-
+        face_x[here, :] = cx
         face_y[here, :] = cy
         face_z[here, :] = cz
         d, e = well_d[here, :], well_e[here, :]
@@ -503,7 +503,10 @@
         )
         return fx
 
-    lax.fori_loop(0, rows, residual_row, zero_row)
+    each_row(residual_row, zero_row)
+
+    own[4] = jnp.max(scale_y.take(own[2]), axis=0)
+    scale_z.start(own.at[4])
 
     def rim_total(before, sat_rim, dtp_rim, weights):
         s = before + dtp_rim * (mobility(sat_rim)[1] * weights)
@@ -524,8 +527,8 @@
         input_x[1, DTP],
         source[pl.ds(cells + cols, cols), :],
     )
-    c = face_x[final, :] * (0.5 * (total[final, :] + t))
-    face_x[final, :] = c
+    c = high_x[...] * (0.5 * (total[final, :] + t))
+    high_x[...] = c
     resid[final, :] -= c * (prs[final, :] - input_x[1, PRS])
     for i, at in ((0, 0), (1, cols - 1)):
         t = rim_total(
@@ -540,10 +543,7 @@
         put(resid, at, edge[i])
 
     def apply(v, b, factor):
-        if factor is not None:
-            v = v * factor
-        high = v.astype(jnp.bfloat16)
-        low = (v - high.astype(jnp.float32)).astype(jnp.bfloat16)
+        high, low = split(v if factor is None else v * factor)
         z = jnp.dot(high, prod_hi[b], preferred_element_type=jnp.float32)
         z += jnp.dot(high, prod_lo[b], preferred_element_type=jnp.float32)
         return z + jnp.dot(low, prod_hi[b], preferred_element_type=jnp.float32)
@@ -584,9 +584,6 @@
         prior = resid if k == 0 else image.at[k - 1]
         precondition_rim(k, prior, edge[0], edge[1], factor)
         send_faces(e)
-        if k == 0:
-            own[4] = jnp.max(scale_y.take(own[2]), axis=0)
-            scale_z.start(own.at[4])
         precondition(prior, vec, factor)
         store = pltpu.make_async_copy(
             vec, (z0_out, z1_out, z2_out)[k], store_sem.at[1 + k]
@@ -608,11 +605,11 @@
             )
             return fx
 
-        lax.fori_loop(0, rows, image_row, zero_row)
+        each_row(image_row, zero_row)
         take_faces(e)
         h = e - 1
         img[first, :] += low_x[...] * (vec[first, :] - halo_x[h, 0])
-        img[final, :] += face_x[final, :] * (vec[final, :] - halo_x[h, 1])
+        img[final, :] += high_x[...] * (vec[final, :] - halo_x[h, 1])
         for i, at in ((0, 0), (1, cols - 1)):
             edge[i] = take(img, at) + side_y[i] * (pack_y[h, i] - halo_y[h, i])
             put(img, at, edge[i])
@@ -711,10 +708,11 @@
             field,
             field,
             pltpu.VMEM((cells + 2 * cols + 2 * rows, 128), f32),
-            pltpu.VMEM((layers, 128), f32),
-            field,
-            field,
-            field,
+            pltpu.VMEM((layers, 128), bf16),
+            field,
+            field,
+            field,
+            pltpu.VMEM((cols, layers), f32),
             pltpu.VMEM((cols, layers), f32),
             pltpu.VMEM((2, rows, layers), f32),
             field,
@@ -735,8 +733,7 @@
             pltpu.VMEM((BASIS, 2, cols, layers), f32),
             pltpu.VMEM((EXCHANGES - 1, 2, rows, layers), f32),
             pltpu.VMEM((7, 1, 128), f32),
-            pltpu.VMEM((2 * REACH + 1, 1, 128), f32),
-            pltpu.VMEM((3, 1, 128), f32),
+            pltpu.VMEM((3 * (2 * REACH + 1), 1, 128), f32),
             pltpu.VMEM((n_gx, 1, 128), f32),
             pltpu.VMEM((n_gy // RING, 1, 128), f32),
             pltpu.VMEM((RING, 1, 128), f32),
@@ -746,8 +743,8 @@
             dma((1 + BASIS,)),
             dma((4,)),
             dma((2, 4)),
-            dma((7,)),
-            dma((7,)),
+            dma((6,)),
+            dma((6,)),
         ]
         operands = (
             jnp.swapaxes(inject_cells, 1, 2),

time: 51.2 us -> 46.2 us (0.902)
  Pallas kernels: 48.7 us -> 43.7 us
    pallas_call x1, Pallas kernels: 48.7 us -> 43.7 us  [per_device(): pl.pallas_call(functools.partial(kernel, (rows, cols, layers, n_gx, n_gy)...]
where the time goes in v5:
time: 46.2 us; the launch traced here: 46.1 us
  Pallas kernels  43.7 us (95%)
  other arithmetic  0.94 us (2%)
  local copies, waits for them, and re-layouts  0.8 us (2%)
  between operations  0.67 us (1%)
    pallas_call x1, Pallas kernels, per_device(): pl.pallas_call(functools.partial(kernel, (rows, cols, layers, n_gx, n_gy)...  43.7 us
    add x1, other arithmetic, per_device(): pressure = pressure_old.reshape(flat) + change  0.94 us

profile of v5, /device:TPU:1, one launch (start us, length us, event | category | flops | bytes accessed | tf_op | source)
XLA Modules:
  0.0 46.1 jit_solution(431290931175140344)
XLA Ops:
  0.6 0.0 copy-start
  0.6 43.7 %reservoir_step.1 = (f32[512,256]{1,0:T(8,128)S(1)}, f32[512,256]{1,0:T(8,128)S(1)}, f32[512,256]{1,0:T(8,128)S(1)}, f32[512,256]{1,0:T(8,128)S(1)}, f32[3,256]{1,0:T(4,128)S(1)}) custom-call(s32[4,2,128]{2,1,0:T(2,128)} %bitcast.19, f32[4]{0:T(128)} %inj_rate.1, s32[8,2,128]{2,1,0:T(2,128)} %bitcast.18, f32[8]{0:T(128)} %pro_pressure.1, f32[8]{0:T(128)} %perm_table.1, ...), custom_call_target="tpu_custom_call" | custom-call | tf_op jit(solution)/shard_map/reservoir_step/pallas_call | solution.py:763
  44.3 0.0 copy-done
  44.3 0.9 %add_add_fusion = f32[512,256]{1,0:T(8,128)} fusion(f32[512,256]{1,0:T(8,128)S(1)} %get-tuple-element.11, f32[512,256]{1,0:T(8,128)S(1)} %get-tuple-element.10, f32[512,256]{1,0:T(8,128)S(1)} %get-tuple-element.9, f32[256]{0:T(256)S(1)} %bitcast.21, f32[256]{0:T(256)S(1)} %bitcast.22, f32[256]{0:T(256)S(1)} %bitcast.20, f32[16,32,256]{2,1,0:T(8,128)S(1)} %copy-done), kind=kLoop, calls=%fused_computation | loop fusion | flops 786432 | bytes 2624512 | tf_op jit(solution)/shard_map/add | solution.py:778
  45.3 0.8 %copy.15 = f32[16,32,256]{2,1,0:T(8,128)} copy(f32[16,32,256]{2,1,0:T(8,128)S(1)} %bitcast.12) | data formatting | bytes 1048576
  (1 shorter events, 0.0 us)
Async XLA Ops:
  0.6 43.7 %copy-start = (f32[16,32,256]{2,1,0:T(8,128)S(1)}, f32[16,32,256]{2,1,0:T(8,128)}, u32[]{:S(2)}) copy-start(f32[16,32,256]{2,1,0:T(8,128)} %param.16) | copy-start | bytes 1572868

commit v6 on v5

--- a/solution.py
+++ b/solution.py
@@ -165,7 +165,8 @@
         if carry is None:
             pl.loop(0, rows // UNROLL)(lambda i: step(i, None) and None)
         else:
-            lax.fori_loop(0, rows // UNROLL, step, carry)
+            carry = lax.fori_loop(0, rows // UNROLL, step, carry)
+        return carry
 
     def split(v):
         high = v.astype(jnp.bfloat16)
@@ -188,7 +189,7 @@
     def greet(peer):
         pl.semaphore_signal(barrier, inc=1, device_id=peer, device_id_type=MESH)
 
-    for peer in plane_peers + window_peers + z_peers:
+    for peer in window_peers[::-1] + plane_peers + z_peers:
         greet(peer)
 
     def clear_x(at):
@@ -366,6 +367,7 @@
 
     each_row(mobility_row)
     spot = spots[...]
+    lane_spot = lax.broadcasted_iota(jnp.int32, (layers, 128), 1)
     picked = sum(product(v, spot, ((1,), (0,))) for v in split(mob[...]))
     own[0] = jnp.sum(picked * select[pl.ds(0, cells), :], axis=0, keepdims=True)
     window.start(own.at[0])
@@ -462,15 +464,24 @@
         pack_y[MOVED - 1, i] = take(moved, c)
     send_faces(MOVED)
 
+    chosen = split(select[...])
+    for w in range(injectors):
+        alone = jnp.where(lane_spot == producers + w, spot, jnp.zeros_like(spot))
+        source[w] = sum(product(v, alone, ((1,), (1,))) for v in chosen)
+
     own[2] = jnp.max(scale_x.take(own[1]), axis=0)
     scale_y.start(own.at[2])
     sums = jnp.sum(window.take(own[0]), axis=0)
     scale = jnp.where(sums > 0.0, rate_row / jnp.where(sums > 0.0, sums, 1.0), 0.0)
-    source[...] = place(select[...] * scale)
+    shares = [scale[:, producers + w : producers + w + 1] for w in range(injectors)]
+
+    def weights(at):
+        return sum(share * source[w, at, :] for w, share in enumerate(shares))
+
 
     def moved_row(x, _):
         here = row(x)
-        made = mob[here, :] * source[here, :]
+        made = mob[here, :] * weights(here)
         s = moved[here, :] + dtp[here, :] * made
         satn[here, :] = s
         resid[here, :] = made
@@ -508,15 +519,15 @@
     own[4] = jnp.max(scale_y.take(own[2]), axis=0)
     scale_z.start(own.at[4])
 
-    def rim_total(before, sat_rim, dtp_rim, weights):
-        s = before + dtp_rim * (mobility(sat_rim)[1] * weights)
+    def rim_total(before, sat_rim, dtp_rim, weight):
+        s = before + dtp_rim * (mobility(sat_rim)[1] * weight)
         return mobility(s)[1]
 
     pack_total = [take(total, 0), take(total, cols - 1)]
     edge = []
     take_faces(MOVED)
     t = rim_total(
-        halo_x[MOVED - 1, 0], input_x[0, SAT], input_x[0, DTP], source[pl.ds(cells, cols), :]
+        halo_x[MOVED - 1, 0], input_x[0, SAT], input_x[0, DTP], weights(pl.ds(cells, cols))
     )
     c = low_x[...] * (0.5 * (total[first, :] + t))
     low_x[...] = c
@@ -525,7 +536,7 @@
         halo_x[MOVED - 1, 1],
         input_x[1, SAT],
         input_x[1, DTP],
-        source[pl.ds(cells + cols, cols), :],
+        weights(pl.ds(cells + cols, cols)),
     )
     c = high_x[...] * (0.5 * (total[final, :] + t))
     high_x[...] = c
@@ -535,7 +546,7 @@
             halo_y[MOVED - 1, i],
             rim[i, SAT],
             rim[i, DTP],
-            source[pl.ds(rim_y + i * rows, rows), :],
+            weights(pl.ds(rim_y + i * rows, rows)),
         )
         c = side_y[i] * (0.5 * (pack_total[i] + t))
         side_y[i] = c
@@ -572,6 +583,27 @@
                 pack_y[BASE - 1 + k, 0] = z[2 * BLOCK : 2 * BLOCK + rows]
             if b == blocks - 1:
                 pack_y[BASE - 1 + k, 1] = z[-rows:]
+
+    pairs = [(0, 0), (1, 0), (1, 1), (2, 0), (2, 1), (2, 2)]
+    count = len(pairs) + BASIS
+    last = len(pairs) - 1
+
+    def fold(total_, term):
+        for i in range(term.shape[0] // 8):
+            total_ = total_ + term[8 * i : 8 * i + 8]
+        return total_
+
+    def dots_row(x, sums):
+        here = row(x)
+        v = [base[k, here, :] for k in range(BASIS)]
+        u = [image[k, here, :] for k in range(BASIS)]
+        r = resid[here, :]
+        terms = [v[i] * u[j] for i, j in pairs] + [v[i] * r for i in range(BASIS)]
+        return tuple(fold(s, term) for s, term in zip(sums, terms))
+
+    def into_lane(i, s, message):
+        s = jnp.sum(s, axis=0, keepdims=True)
+        return jnp.where(lane == i, jnp.sum(s, axis=1, keepdims=True), message)
 
     stores = [store_satn]
     for k in range(BASIS):
@@ -606,36 +638,27 @@
             return fx
 
         each_row(image_row, zero_row)
+        h = e - 1
+        if k < BASIS - 1:
+            take_faces(e)
+            img[first, :] += low_x[...] * (vec[first, :] - halo_x[h, 0])
+            img[final, :] += high_x[...] * (vec[final, :] - halo_x[h, 1])
+            for i, at in ((0, 0), (1, cols - 1)):
+                edge[i] = take(img, at) + side_y[i] * (pack_y[h, i] - halo_y[h, i])
+                put(img, at, edge[i])
+            continue
+        sums = each_row(dots_row, (jnp.zeros((8, layers), jnp.float32),) * count)
+        message = jnp.zeros((1, 128), jnp.float32)
+        for i, s in enumerate(sums):
+            if i != last:
+                message = into_lane(i, s, message)
         take_faces(e)
-        h = e - 1
-        img[first, :] += low_x[...] * (vec[first, :] - halo_x[h, 0])
-        img[final, :] += high_x[...] * (vec[final, :] - halo_x[h, 1])
-        for i, at in ((0, 0), (1, cols - 1)):
-            edge[i] = take(img, at) + side_y[i] * (pack_y[h, i] - halo_y[h, i])
-            put(img, at, edge[i])
-
-    pairs = [(0, 0), (1, 0), (1, 1), (2, 0), (2, 1), (2, 2)]
-
-    def dots_row(x, sums):
-        here = row(x)
-        v = [base[k, here, :] for k in range(BASIS)]
-        u = [image[k, here, :] for k in range(BASIS)]
-        r = resid[here, :]
-        terms = [v[i] * u[j] for i, j in pairs] + [v[i] * r for i in range(BASIS)]
-        out = []
-        for s, term in zip(sums, terms):
-            for i in range(cols // 8):
-                s = s + term[8 * i : 8 * i + 8]
-            out.append(s)
-        return tuple(out)
-
-    zero_sum = jnp.zeros((8, layers), jnp.float32)
-    count = len(pairs) + BASIS
-    sums = lax.fori_loop(0, rows, dots_row, (zero_sum,) * count)
-    message = jnp.zeros((1, 128), jnp.float32)
-    for i, s in enumerate(sums):
-        s = jnp.sum(s, axis=0, keepdims=True)
-        message = jnp.where(lane == i, jnp.sum(s, axis=1, keepdims=True), message)
+        s = fold(sums[last], low_x[...] * (vec[first, :] - halo_x[h, 0]) * vec[first, :])
+        s = fold(s, high_x[...] * (vec[final, :] - halo_x[h, 1]) * vec[final, :])
+        for i in range(2):
+            s = fold(s, side_y[i] * (pack_y[h, i] - halo_y[h, i]) * pack_y[h, i])
+        message = into_lane(last, s, message)
+
     own[5] = message
     sum_plane.start(own.at[5])
     own[6] = jnp.sum(sum_plane.take(own[5]), axis=0)
@@ -718,7 +741,9 @@
             field,
             field,
             field,
-            pltpu.VMEM((cells + 2 * cols + 2 * rows, layers), f32),
+            pltpu.VMEM(
+                (inject_index.shape[0], cells + 2 * cols + 2 * rows, layers), f32
+            ),
             field,
             field,
             field,

time: 46.2 us -> 45.5 us (0.985)
  Pallas kernels: 43.7 us -> 42.9 us
    pallas_call x1, Pallas kernels: 43.7 us -> 42.9 us  [per_device(): pl.pallas_call(functools.partial(kernel, (rows, cols, layers, n_gx, n_gy)...]
where the time goes in v6:
time: 45.5 us; the launch traced here: 45.3 us
  Pallas kernels  42.9 us (94%)
  other arithmetic  0.94 us (2%)
  local copies, waits for them, and re-layouts  0.8 us (2%)
  between operations  0.67 us (1%)
    pallas_call x1, Pallas kernels, per_device(): pl.pallas_call(functools.partial(kernel, (rows, cols, layers, n_gx, n_gy)...  42.9 us
    add x1, other arithmetic, per_device(): pressure = pressure_old.reshape(flat) + change  0.94 us

profile of v6, /device:TPU:1, one launch (start us, length us, event | category | flops | bytes accessed | tf_op | source)
XLA Modules:
  0.0 45.3 jit_solution(4671580771646385605)
XLA Ops:
  0.6 0.0 copy-start
  0.6 42.9 %reservoir_step.1 = (f32[512,256]{1,0:T(8,128)S(1)}, f32[512,256]{1,0:T(8,128)S(1)}, f32[512,256]{1,0:T(8,128)S(1)}, f32[512,256]{1,0:T(8,128)S(1)}, f32[3,256]{1,0:T(4,128)S(1)}) custom-call(s32[4,2,128]{2,1,0:T(2,128)} %bitcast.19, f32[4]{0:T(128)} %inj_rate.1, s32[8,2,128]{2,1,0:T(2,128)} %bitcast.18, f32[8]{0:T(128)} %pro_pressure.1, f32[8]{0:T(128)} %perm_table.1, ...), custom_call_target="tpu_custom_call" | custom-call | tf_op jit(solution)/shard_map/reservoir_step/pallas_call | solution.py:788
  43.6 0.0 copy-done
  43.6 0.9 %add_add_fusion = f32[512,256]{1,0:T(8,128)} fusion(f32[512,256]{1,0:T(8,128)S(1)} %get-tuple-element.11, f32[512,256]{1,0:T(8,128)S(1)} %get-tuple-element.10, f32[512,256]{1,0:T(8,128)S(1)} %get-tuple-element.9, f32[256]{0:T(256)S(1)} %bitcast.21, f32[256]{0:T(256)S(1)} %bitcast.22, f32[256]{0:T(256)S(1)} %bitcast.20, f32[16,32,256]{2,1,0:T(8,128)S(1)} %copy-done), kind=kLoop, calls=%fused_computation | loop fusion | flops 786432 | bytes 2624512 | tf_op jit(solution)/shard_map/add | solution.py:803
  44.5 0.8 %copy.15 = f32[16,32,256]{2,1,0:T(8,128)} copy(f32[16,32,256]{2,1,0:T(8,128)S(1)} %bitcast.12) | data formatting | bytes 1048576
  (1 shorter events, 0.0 us)
Async XLA Ops:
  0.6 43.0 %copy-start = (f32[16,32,256]{2,1,0:T(8,128)S(1)}, f32[16,32,256]{2,1,0:T(8,128)}, u32[]{:S(2)}) copy-start(f32[16,32,256]{2,1,0:T(8,128)} %param.16) | copy-start | bytes 1572868

commit v7 on v6

--- a/solution.py
+++ b/solution.py
@@ -97,6 +97,8 @@
     store_sem,
     face_send,
     face_recv,
+    late_send,
+    late_recv,
     group_send,
     group_recv,
 ):
@@ -124,10 +126,6 @@
         parts = [ref[pl.ds(x * cols + c, 1), :] for x in range(rows)]
         return jnp.concatenate(parts, axis=0)
 
-    def add_to(ref, c, value):
-        for x in range(rows):
-            ref[pl.ds(x * cols + c, 1), :] += value[x : x + 1]
-
     def put(ref, c, value):
         for x in range(rows):
             ref[pl.ds(x * cols + c, 1), :] = value[x : x + 1]
@@ -236,11 +234,12 @@
 
     def face_copy(e, d):
         if e == INPUT:
+            soon = pl.ds(0, DTP)
             if d < 2:
-                src = inp.at[:, pl.ds(0 if d == LO_X else cells - cols, cols), :]
-                dst = input_x.at[1 - d]
+                src = inp.at[soon, pl.ds(0 if d == LO_X else cells - cols, cols), :]
+                dst = input_x.at[1 - d, soon]
             else:
-                src, dst = input_pack.at[d - 2], input_y.at[3 - d]
+                src, dst = input_pack.at[d - 2, soon], input_y.at[3 - d, soon]
         else:
             if d < 2:
                 at = pl.ds(0 if d == LO_X else cells - cols, cols)
@@ -270,6 +269,21 @@
         for d in range(4):
             pl.when(hears[d])(lambda: face_copy(e, d).wait_recv())
 
+    def late_copy(d):
+        if d < 2:
+            src = dtp.at[pl.ds(0 if d == LO_X else cells - cols, cols), :]
+            dst = input_x.at[1 - d, DTP]
+        else:
+            src, dst = input_pack.at[d - 2, DTP], input_y.at[3 - d, DTP]
+        return pltpu.make_async_remote_copy(
+            src_ref=src,
+            dst_ref=dst,
+            send_sem=late_send.at[d],
+            recv_sem=late_recv.at[d],
+            device_id=neighbours[d],
+            device_id_type=MESH,
+        )
+
     class Group:
         def __init__(self, k, peers, slots):
             self.k, self.peers, self.slots = k, peers, slots
@@ -307,6 +321,8 @@
 
     pl.semaphore_wait(barrier, len(plane_peers) + len(window_peers) + len(z_peers))
     send_faces(INPUT)
+    for d in range(4):
+        pl.when(sends[d])(lambda: late_copy(d).start())
 
     lane = lax.broadcasted_iota(jnp.int32, (1, 128), 1)
     well_row = jnp.full((1, 128), -9, jnp.int32)
@@ -455,22 +471,23 @@
     t = harmonic(rim[0, PERM], pack[0, PERM])
     side_y[0] = t
     flux = upwind(t, rim[0, PRS], pack[0, PRS], fraction(rim[0, SAT]), fraction(pack[0, SAT]))
-    add_to(moved, 0, pack[0, DTP] * flux)
+    rims = [take(moved, 0) + pack[0, DTP] * flux]
     t = harmonic(pack[1, PERM], rim[1, PERM])
     side_y[1] = t
     flux = upwind(t, pack[1, PRS], rim[1, PRS], fraction(pack[1, SAT]), fraction(rim[1, SAT]))
-    add_to(moved, cols - 1, -pack[1, DTP] * flux)
+    rims.append(take(moved, cols - 1) - pack[1, DTP] * flux)
     for i, c in ((0, 0), (1, cols - 1)):
-        pack_y[MOVED - 1, i] = take(moved, c)
+        pack_y[MOVED - 1, i] = rims[i]
+        put(moved, c, rims[i])
     send_faces(MOVED)
+    own[2] = jnp.max(scale_x.take(own[1]), axis=0)
+    scale_y.start(own.at[2])
 
     chosen = split(select[...])
     for w in range(injectors):
         alone = jnp.where(lane_spot == producers + w, spot, jnp.zeros_like(spot))
         source[w] = sum(product(v, alone, ((1,), (1,))) for v in chosen)
 
-    own[2] = jnp.max(scale_x.take(own[1]), axis=0)
-    scale_y.start(own.at[2])
     sums = jnp.sum(window.take(own[0]), axis=0)
     scale = jnp.where(sums > 0.0, rate_row / jnp.where(sums > 0.0, sums, 1.0), 0.0)
     shares = [scale[:, producers + w : producers + w + 1] for w in range(injectors)]
@@ -526,6 +543,8 @@
     pack_total = [take(total, 0), take(total, cols - 1)]
     edge = []
     take_faces(MOVED)
+    for d in range(4):
+        pl.when(hears[d])(lambda: late_copy(d).wait_recv())
     t = rim_total(
         halo_x[MOVED - 1, 0], input_x[0, SAT], input_x[0, DTP], weights(pl.ds(cells, cols))
     )
@@ -688,6 +707,7 @@
         group.whole().wait_send()
     for d in range(4):
         pl.when(sends[d])(lambda: face_copy(EXCHANGES - 1, d).wait_send())
+        pl.when(sends[d])(lambda: late_copy(d).wait_send())
     for store in stores:
         store.wait()
 
@@ -768,6 +788,8 @@
             dma((1 + BASIS,)),
             dma((4,)),
             dma((2, 4)),
+            dma((4,)),
+            dma((4,)),
             dma((6,)),
             dma((6,)),
         ]

time: 45.5 us -> 45.5 us (level)
  no operation moved by 1% of the time
where the time goes in v7:
time: 45.5 us; the launch traced here: 45.4 us
  Pallas kernels  43 us (95%)
  other arithmetic  0.94 us (2%)
  local copies, waits for them, and re-layouts  0.8 us (2%)
  between operations  0.67 us (1%)
    pallas_call x1, Pallas kernels, per_device(): pl.pallas_call(functools.partial(kernel, (rows, cols, layers, n_gx, n_gy)...  43 us
    add x1, other arithmetic, per_device(): pressure = pressure_old.reshape(flat) + change  0.94 us

profile of v7, /device:TPU:1, one launch (start us, length us, event | category | flops | bytes accessed | tf_op | source)
XLA Modules:
  0.0 45.4 jit_solution(10991191160484762625)
XLA Ops:
  0.6 0.0 copy-start
  0.6 43.0 %reservoir_step.1 = (f32[512,256]{1,0:T(8,128)S(1)}, f32[512,256]{1,0:T(8,128)S(1)}, f32[512,256]{1,0:T(8,128)S(1)}, f32[512,256]{1,0:T(8,128)S(1)}, f32[3,256]{1,0:T(4,128)S(1)}) custom-call(s32[4,2,128]{2,1,0:T(2,128)} %bitcast.19, f32[4]{0:T(128)} %inj_rate.1, s32[8,2,128]{2,1,0:T(2,128)} %bitcast.18, f32[8]{0:T(128)} %pro_pressure.1, f32[8]{0:T(128)} %perm_table.1, ...), custom_call_target="tpu_custom_call" | custom-call | tf_op jit(solution)/shard_map/reservoir_step/pallas_call | solution.py:810
  43.7 0.0 copy-done
  43.7 0.9 %add_add_fusion = f32[512,256]{1,0:T(8,128)} fusion(f32[512,256]{1,0:T(8,128)S(1)} %get-tuple-element.11, f32[512,256]{1,0:T(8,128)S(1)} %get-tuple-element.10, f32[512,256]{1,0:T(8,128)S(1)} %get-tuple-element.9, f32[256]{0:T(256)S(1)} %bitcast.21, f32[256]{0:T(256)S(1)} %bitcast.22, f32[256]{0:T(256)S(1)} %bitcast.20, f32[16,32,256]{2,1,0:T(8,128)S(1)} %copy-done), kind=kLoop, calls=%fused_computation | loop fusion | flops 786432 | bytes 2624512 | tf_op jit(solution)/shard_map/add | solution.py:825
  44.6 0.8 %copy.15 = f32[16,32,256]{2,1,0:T(8,128)} copy(f32[16,32,256]{2,1,0:T(8,128)S(1)} %bitcast.12) | data formatting | bytes 1048576
  (1 shorter events, 0.0 us)
Async XLA Ops:
  0.6 43.0 %copy-start = (f32[16,32,256]{2,1,0:T(8,128)S(1)}, f32[16,32,256]{2,1,0:T(8,128)}, u32[]{:S(2)}) copy-start(f32[16,32,256]{2,1,0:T(8,128)} %param.16) | copy-start | bytes 1572868

commit v8 on v7

--- a/solution.py
+++ b/solution.py
@@ -19,7 +19,6 @@
 EXCHANGES = BASE + BASIS
 SAT, PRS, PERM, DTP = 0, 1, 2, 3
 LO_X, HI_X, LO_Y, HI_Y = 0, 1, 2, 3
-REACH = 5
 FAR_X = (4, 3, 5, 2, 6, 1, 7)
 FAR_Y = (2, 1, 3)
 FAR_Z = (4, 3, 5, 2, 6, 1, 7)
@@ -88,6 +87,7 @@
     pack_y,
     own,
     slot_w,
+    slot_v,
     slot_x,
     slot_y,
     slot_s,
@@ -144,11 +144,9 @@
         z = lax.rem(zz + c, RING) if c else zz
         return (lax.rem(gx + a, n_gx) if a else gx, y * RING + z)
 
-    def line(a, b):
-        return (lax.rem(gx + n_gx + a, n_gx), lax.rem(gy + n_gy + b, n_gy))
-
-    reach = [b for d in range(REACH, 0, -1) for b in (d, -d)] + [0]
-    window_peers = [line(a, b) for b in reach for a in (-1, 1, 0) if a or b]
+    around_peers = [
+        near(a, b) for a in (n_gx - 1, 1, 0) for b in (n_y - 1, 1, 0) if a or b
+    ]
     x_peers = [near(a, 0) for a in FAR_X]
     y_peers = [near(0, b) for b in FAR_Y]
     z_peers = [near(0, 0, c) for c in FAR_Z]
@@ -187,7 +185,7 @@
     def greet(peer):
         pl.semaphore_signal(barrier, inc=1, device_id=peer, device_id_type=MESH)
 
-    for peer in window_peers[::-1] + plane_peers + z_peers:
+    for peer in neighbours[2:] + tuple(plane_peers[::-1]) + tuple(z_peers[::-1]):
         greet(peer)
 
     def clear_x(at):
@@ -311,15 +309,16 @@
             self.slots[len(self.peers)] = mine
             return self.slots[...]
 
-    window = Group(0, window_peers, slot_w)
+    well_z = Group(0, z_peers, slot_v)
+    well_xy = Group(6, around_peers, slot_w)
     scale_x = Group(1, x_peers, slot_x)
     scale_y = Group(2, y_peers, slot_y)
     scale_z = Group(3, z_peers, slot_s)
     sum_plane = Group(4, plane_peers, slot_a)
     sum_z = Group(5, z_peers, slot_b)
-    groups = (window, scale_x, scale_y, scale_z, sum_plane, sum_z)
-
-    pl.semaphore_wait(barrier, len(plane_peers) + len(window_peers) + len(z_peers))
+    groups = (well_z, well_xy, scale_x, scale_y, scale_z, sum_plane, sum_z)
+
+    pl.semaphore_wait(barrier, 2 + len(plane_peers) + len(z_peers))
     send_faces(INPUT)
     for d in range(4):
         pl.when(sends[d])(lambda: late_copy(d).start())
@@ -386,7 +385,7 @@
     lane_spot = lax.broadcasted_iota(jnp.int32, (layers, 128), 1)
     picked = sum(product(v, spot, ((1,), (0,))) for v in split(mob[...]))
     own[0] = jnp.sum(picked * select[pl.ds(0, cells), :], axis=0, keepdims=True)
-    window.start(own.at[0])
+    well_z.start(own.at[0])
 
     lane_z = lax.broadcasted_iota(jnp.int32, (cols, layers), 1)
     col_y = lax.broadcasted_iota(jnp.int32, (cols, layers), 0)
@@ -480,6 +479,8 @@
         pack_y[MOVED - 1, i] = rims[i]
         put(moved, c, rims[i])
     send_faces(MOVED)
+    own[3] = jnp.sum(well_z.take(own[0]), axis=0)
+    well_xy.start(own.at[3])
     own[2] = jnp.max(scale_x.take(own[1]), axis=0)
     scale_y.start(own.at[2])
 
@@ -488,7 +489,7 @@
         alone = jnp.where(lane_spot == producers + w, spot, jnp.zeros_like(spot))
         source[w] = sum(product(v, alone, ((1,), (1,))) for v in chosen)
 
-    sums = jnp.sum(window.take(own[0]), axis=0)
+    sums = jnp.sum(well_xy.take(own[3]), axis=0)
     scale = jnp.where(sums > 0.0, rate_row / jnp.where(sums > 0.0, sums, 1.0), 0.0)
     shares = [scale[:, producers + w : producers + w + 1] for w in range(injectors)]
 
@@ -778,7 +779,8 @@
             pltpu.VMEM((BASIS, 2, cols, layers), f32),
             pltpu.VMEM((EXCHANGES - 1, 2, rows, layers), f32),
             pltpu.VMEM((7, 1, 128), f32),
-            pltpu.VMEM((3 * (2 * REACH + 1), 1, 128), f32),
+            pltpu.VMEM((9, 1, 128), f32),
+            pltpu.VMEM((RING, 1, 128), f32),
             pltpu.VMEM((n_gx, 1, 128), f32),
             pltpu.VMEM((n_gy // RING, 1, 128), f32),
             pltpu.VMEM((RING, 1, 128), f32),
@@ -790,8 +792,8 @@
             dma((2, 4)),
             dma((4,)),
             dma((4,)),
-            dma((6,)),
-            dma((6,)),
+            dma((7,)),
+            dma((7,)),
         ]
         operands = (
             jnp.swapaxes(inject_cells, 1, 2),

time: 45.5 us -> 45.4 us (level)
  no operation moved by 1% of the time
where the time goes in v8:
time: 45.4 us; the launch traced here: 45.2 us
  Pallas kernels  42.8 us (94%)
  other arithmetic  0.94 us (2%)
  local copies, waits for them, and re-layouts  0.8 us (2%)
  between operations  0.67 us (1%)
    pallas_call x1, Pallas kernels, per_device(): pl.pallas_call(functools.partial(kernel, (rows, cols, layers, n_gx, n_gy)...  42.8 us
    add x1, other arithmetic, per_device(): pressure = pressure_old.reshape(flat) + change  0.94 us

profile of v8, /device:TPU:1, one launch (start us, length us, event | category | flops | bytes accessed | tf_op | source)
XLA Modules:
  0.0 45.2 jit_solution(14556229732786874341)
XLA Ops:
  0.6 0.0 copy-start
  0.6 42.8 %reservoir_step.1 = (f32[512,256]{1,0:T(8,128)S(1)}, f32[512,256]{1,0:T(8,128)S(1)}, f32[512,256]{1,0:T(8,128)S(1)}, f32[512,256]{1,0:T(8,128)S(1)}, f32[3,256]{1,0:T(4,128)S(1)}) custom-call(s32[4,2,128]{2,1,0:T(2,128)} %bitcast.19, f32[4]{0:T(128)} %inj_rate.1, s32[8,2,128]{2,1,0:T(2,128)} %bitcast.18, f32[8]{0:T(128)} %pro_pressure.1, f32[8]{0:T(128)} %perm_table.1, ...), custom_call_target="tpu_custom_call" | custom-call | tf_op jit(solution)/shard_map/reservoir_step/pallas_call | solution.py:812
  43.5 0.0 copy-done
  43.5 0.9 %add_add_fusion = f32[512,256]{1,0:T(8,128)} fusion(f32[512,256]{1,0:T(8,128)S(1)} %get-tuple-element.11, f32[512,256]{1,0:T(8,128)S(1)} %get-tuple-element.10, f32[512,256]{1,0:T(8,128)S(1)} %get-tuple-element.9, f32[256]{0:T(256)S(1)} %bitcast.21, f32[256]{0:T(256)S(1)} %bitcast.22, f32[256]{0:T(256)S(1)} %bitcast.20, f32[16,32,256]{2,1,0:T(8,128)S(1)} %copy-done), kind=kLoop, calls=%fused_computation | loop fusion | flops 786432 | bytes 2624512 | tf_op jit(solution)/shard_map/add | solution.py:827
  44.4 0.8 %copy.15 = f32[16,32,256]{2,1,0:T(8,128)} copy(f32[16,32,256]{2,1,0:T(8,128)S(1)} %bitcast.12) | data formatting | bytes 1048576
  (1 shorter events, 0.0 us)
Async XLA Ops:
  0.6 42.9 %copy-start = (f32[16,32,256]{2,1,0:T(8,128)S(1)}, f32[16,32,256]{2,1,0:T(8,128)}, u32[]{:S(2)}) copy-start(f32[16,32,256]{2,1,0:T(8,128)} %param.16) | copy-start | bytes 1572868

commit v9 on v8

--- a/solution.py
+++ b/solution.py
@@ -11,6 +11,7 @@
 BLOCK = 16
 BASIS = 3
 UNROLL = 4
+CHUNKS = 4
 RING = 8
 TIME_STEP = 0.002
 SHIFT = 2.0**-14
@@ -713,6 +714,22 @@
         store.wait()
 
 
+def closing(coef, prs, z0, z1, z2, satn, satn_out, out, result, sems):
+    stores = [pltpu.make_async_copy(satn, satn_out, sems.at[CHUNKS])]
+    stores[0].start()
+    size = prs.shape[0] // CHUNKS
+    for i in range(CHUNKS):
+        at = pl.ds(i * size, size)
+        result[at, :] = prs[at, :] + (
+            coef[0:1, :] * z0[at, :] + coef[1:2, :] * z1[at, :] + coef[2:3, :] * z2[at, :]
+        )
+        store = pltpu.make_async_copy(result.at[at], out.at[at], sems.at[i])
+        store.start()
+        stores.append(store)
+    for store in stores:
+        store.wait()
+
+
 def solution(mesh):
     n_gx, n_gy = mesh.shape["gx"], mesh.shape["gy"]
 
@@ -823,8 +840,15 @@
             ),
             name="reservoir_step",
         )(*(pltpu.with_memory_space_constraint(a, pltpu.HBM) for a in operands))
-        change = coef[0:1] * z0 + coef[1:2] * z1 + coef[2:3] * z2
-        pressure = pressure_old.reshape(flat) + change
+        satn, pressure = pl.pallas_call(
+            closing,
+            out_shape=[jax.ShapeDtypeStruct(flat, f32)] * 2,
+            in_specs=[vmem] * 5 + [out],
+            out_specs=[hbm] * 2,
+            scratch_shapes=[field, dma((CHUNKS + 1,))],
+            compiler_params=pltpu.CompilerParams(vmem_limit_bytes=8 * 1024 * 1024),
+            name="reservoir_close",
+        )(coef, pressure_old.reshape(flat), z0, z1, z2, satn)
         return satn.reshape(saturation.shape), pressure.reshape(saturation.shape)
 
     grid = P("gx", "gy", None)

time: 45.4 us -> 44.6 us (0.982)
  Pallas kernels: 42.8 us -> 43.8 us
  other arithmetic: 0.94 us -> 0 us
  local copies, waits for them, and re-layouts: 0.8 us -> 0.01 us
    pallas_call x0 -> x1, Pallas kernels: none -> 1 us  [per_device(): pl.pallas_call(closing, out_shape=[jax.ShapeDtypeStruct(flat, f32)] * 2,...]
    add x1 -> x0, other arithmetic: 0.94 us -> none  [per_device(): pressure = pressure_old.reshape(flat) + change]
    unnamed x3 -> x2, local copies, waits for them, and re-layouts: 0.8 us -> 0.01 us
where the time goes in v9:
time: 44.6 us; the launch traced here: 44.5 us
  Pallas kernels  43.8 us (98%)
  between operations  0.66 us (1%)
    pallas_call x1, Pallas kernels, per_device(): pl.pallas_call(functools.partial(kernel, (rows, cols, layers, n_gx, n_gy)...  42.8 us
    pallas_call x1, Pallas kernels, per_device(): pl.pallas_call(closing, out_shape=[jax.ShapeDtypeStruct(flat, f32)] * 2,...  1 us

profile of v9, /device:TPU:1, one launch (start us, length us, event | category | flops | bytes accessed | tf_op | source)
XLA Modules:
  0.0 44.5 jit_solution(4602263863222205198)
XLA Ops:
  0.6 0.0 copy-start
  0.6 42.8 %reservoir_step.1 = (f32[512,256]{1,0:T(8,128)S(1)}, f32[512,256]{1,0:T(8,128)S(1)}, f32[512,256]{1,0:T(8,128)S(1)}, f32[512,256]{1,0:T(8,128)S(1)}, f32[3,256]{1,0:T(4,128)S(1)}) custom-call(s32[4,2,128]{2,1,0:T(2,128)} %bitcast.14, f32[4]{0:T(128)} %inj_rate.1, s32[8,2,128]{2,1,0:T(2,128)} %bitcast.13, f32[8]{0:T(128)} %pro_pressure.1, f32[8]{0:T(128)} %perm_table.1, ...), custom_call_target="tpu_custom_call" | custom-call | tf_op jit(solution)/shard_map/reservoir_step/pallas_call | solution.py:829
  43.5 0.0 copy-done
  43.5 1.0 %reservoir_close.1 = (f32[512,256]{1,0:T(8,128)}, f32[512,256]{1,0:T(8,128)}) custom-call(f32[3,256]{1,0:T(4,128)S(1)} %get-tuple-element.9.coef, f32[512,256]{1,0:T(8,128)S(1)} %bitcast.9, f32[512,256]{1,0:T(8,128)S(1)} %get-tuple-element.10.z0, f32[512,256]{1,0:T(8,128)S(1)} %get-tuple-element.11.z1, f32[512,256]{1,0:T(8,128)S(1)} %get-tuple-element.12.z2, ...), custom_call_target="tpu_custom_call" | custom-call | tf_op jit(solution)/shard_map/reservoir_close/pallas_call | solution.py:843
Async XLA Ops:
  0.6 42.8 %copy-start = (f32[16,32,256]{2,1,0:T(8,128)S(1)}, f32[16,32,256]{2,1,0:T(8,128)}, u32[]{:S(2)}) copy-start(f32[16,32,256]{2,1,0:T(8,128)} %param.16) | copy-start | bytes 1572868

commit v10 on v9

--- a/solution.py
+++ b/solution.py
@@ -10,7 +10,7 @@
 MESH = pl.DeviceIdType.MESH
 BLOCK = 16
 BASIS = 3
-UNROLL = 4
+UNROLL = 8
 CHUNKS = 4
 RING = 8
 TIME_STEP = 0.002

time: 44.6 us -> 44.3 us (level)
  no operation moved by 1% of the time
where the time goes in v10:
time: 44.3 us; the launch traced here: 44.2 us
  Pallas kernels  43.5 us (98%)
  between operations  0.66 us (1%)
    pallas_call x1, Pallas kernels, per_device(): pl.pallas_call(functools.partial(kernel, (rows, cols, layers, n_gx, n_gy)...  42.5 us
    pallas_call x1, Pallas kernels, per_device(): pl.pallas_call(closing, out_shape=[jax.ShapeDtypeStruct(flat, f32)] * 2,...  1 us

profile of v10, /device:TPU:1, one launch (start us, length us, event | category | flops | bytes accessed | tf_op | source)
XLA Modules:
  0.0 44.2 jit_solution(15973883688717878833)
XLA Ops:
  0.6 0.0 copy-start
  0.6 42.5 %reservoir_step.1 = (f32[512,256]{1,0:T(8,128)S(1)}, f32[512,256]{1,0:T(8,128)S(1)}, f32[512,256]{1,0:T(8,128)S(1)}, f32[512,256]{1,0:T(8,128)S(1)}, f32[3,256]{1,0:T(4,128)S(1)}) custom-call(s32[4,2,128]{2,1,0:T(2,128)} %bitcast.14, f32[4]{0:T(128)} %inj_rate.1, s32[8,2,128]{2,1,0:T(2,128)} %bitcast.13, f32[8]{0:T(128)} %pro_pressure.1, f32[8]{0:T(128)} %perm_table.1, ...), custom_call_target="tpu_custom_call" | custom-call | tf_op jit(solution)/shard_map/reservoir_step/pallas_call | solution.py:829
  43.2 0.0 copy-done
  43.2 1.0 %reservoir_close.1 = (f32[512,256]{1,0:T(8,128)}, f32[512,256]{1,0:T(8,128)}) custom-call(f32[3,256]{1,0:T(4,128)S(1)} %get-tuple-element.9.coef, f32[512,256]{1,0:T(8,128)S(1)} %bitcast.9, f32[512,256]{1,0:T(8,128)S(1)} %get-tuple-element.10.z0, f32[512,256]{1,0:T(8,128)S(1)} %get-tuple-element.11.z1, f32[512,256]{1,0:T(8,128)S(1)} %get-tuple-element.12.z2, ...), custom_call_target="tpu_custom_call" | custom-call | tf_op jit(solution)/shard_map/reservoir_close/pallas_call | solution.py:843
Async XLA Ops:
  0.6 42.6 %copy-start = (f32[16,32,256]{2,1,0:T(8,128)S(1)}, f32[16,32,256]{2,1,0:T(8,128)}, u32[]{:S(2)}) copy-start(f32[16,32,256]{2,1,0:T(8,128)} %param.16) | copy-start | bytes 1572868
